TPU v7x, 128 devices: a whole 4x4x4 slice. The times are simulated.
128 devices in a mesh: kxy: 16 (over z_lo, y, core), kz: 8 (over z_hi, x).
Axes of the slice: x: 4, y: 4, z: 4 (z_hi: 2, z_lo: 2; z = z_hi * 2 + z_lo), core: 2. Of those that a mesh axis runs over, the one named last changes fastest.
Arguments:
- factors: float32 [16, 8, 2, 384, 1024], P('kxy', 'kz'), may hold values from -0.9 to 0.9
- occ_energy: float32 [16, 8, 8], P('kxy', 'kz'), may hold values from -2 to -0.5
- vir_energy: float32 [16, 8, 128], P('kxy', 'kz'), may hold values from 0.5 to 3
- shifts: int32 [2, 2], replicated, may hold values from 0 to 3, as said below
Outputs:
- gradient: float32 [16, 8, 2, 384, 1024], P('kxy', 'kz')
Inputs may be any that keep to these rules, and one draw needn't show every extreme that they name: `shifts`: row 0 (the momentum transfer) has both entries between 1 and 3. Row 1 is the partner displacement; it is always (3, 3).
All inputs are finite; a program needn't handle non-finite values.
Results may differ from a plain program's by a relative error of at most 0.0001.
Values sent between devices are 32-bit elements; how exact they have to be, the bound alone decides.
No kernel may reach another device: no remote copies, remote signals or barrier semaphores. Data moves between devices by JAX's collectives and lax.ppermute only.
A program may use at most 64 MiB of HBM per device.

v0:
```python
import functools

import jax
import jax.numpy as jnp
from jax import lax
from jax.experimental import pallas as pl
from jax.experimental.pallas import tpu as pltpu
from jax.sharding import PartitionSpec as P


REACH = 4
LIMIT = 26 << 20
AXES = ("kxy", "kz")
MEET_Z = ((0, 0, 1, 1), (3, 2, 3, 3), (3, 2, 3, 3), (1, 0, 0, 0))


def coordinates(kx, kz):
    return kz % 4, (kx // 2) % 4, 2 * (kz // 4) + kx // 8


def device(x, y, z, core):
    return (8 * (z % 2) + 2 * (y % 4) + core) * 8 + 4 * (z // 2) + x


def routes(count_x, count_z):
    odd, after, before = {}, {}, {}
    for kx in range(1, count_x, 2):
        for kz in range(count_z):
            x, y, z = coordinates(kx, kz)
            meet = (x, y - 1, z ^ MEET_Z[x][y])
            odd[kx * count_z + kz] = meet
            after[(kx + 3) % count_x * count_z + (kz + 3) % count_z] = meet
            before[(kx - 3) % count_x * count_z + (kz - 3) % count_z] = meet
    return odd, after, before


def onto(meets, core):
    return {source: device(*meet, core) for source, meet in meets.items()}


def move(x, route):
    return lax.ppermute(x, AXES, sorted(route.items()))


def move_back(x, route):
    return lax.ppermute(x, AXES, sorted((t, s) for s, t in route.items()))


def split(x):
    high = x.astype(jnp.bfloat16)
    return high, (x - high.astype(jnp.float32)).astype(jnp.bfloat16)


def left(x, axis):
    high, low = split(x)
    return jnp.concatenate([high, high, low], axis)


def right(x, axis):
    high, low = split(x)
    return jnp.concatenate([high, low, high], axis)


def product(x, y, inner_x, inner_y):
    return lax.dot_general(
        x, y, (((inner_x,), (inner_y,)), ((), ())), preferred_element_type=jnp.float32
    )


def block_kernel(has_o, has_w, *refs):
    o_ref, w_ref, gap_o_ref, gap_w_ref, *refs = refs
    old_o = refs.pop(0) if has_o else None
    old_w = refs.pop(0) if has_w else None
    to_o, to_w, tall, flat = refs
    a, b = o_ref[0], o_ref[1]
    inner = a.shape[0]
    for i, x in enumerate((a, b, a + b)):
        flat[i] = left(x, 1)
        high, low = split(x.T)
        tall[i, :, :inner] = high
        tall[i, :, inner : 2 * inner] = high
        tall[i, :, 2 * inner :] = low
    c, d = w_ref[0], w_ref[1]
    ac = product(tall[0], right(c, 0), 1, 0)
    bd = product(tall[1], right(d, 0), 1, 0)
    both = product(tall[2], right(c - d, 0), 1, 0)
    inverse = 1.0 / (gap_o_ref[...] + gap_w_ref[...])
    p = (ac + bd) * inverse
    q = (both - ac + bd) * inverse
    cp = product(left(c, 1), right(p, 1), 1, 1)
    dq = product(left(d, 1), right(q, 1), 1, 1)
    both = product(left(c + d, 1), right(p + q, 1), 1, 1)
    re, im = cp - dq, both - cp - dq
    to_o[0] = re + old_o[0] if has_o else re
    to_o[1] = im + old_o[1] if has_o else im
    ap = product(flat[0], right(p, 0), 1, 0)
    bq = product(flat[1], right(q, 0), 1, 0)
    both = product(flat[2], right(p - q, 0), 1, 0)
    re, im = ap + bq, both - ap + bq
    to_w[0] = re + old_w[0] if has_w else re
    to_w[1] = im + old_w[1] if has_w else im


def block(o, w, gap_o, gap_w, old_o=None, old_w=None):
    inner, m = o.shape[1:]
    n = w.shape[2]
    old = [x for x in (old_o, old_w) if x is not None]
    spec = pl.BlockSpec(memory_space=pltpu.VMEM)
    return pl.pallas_call(
        functools.partial(block_kernel, old_o is not None, old_w is not None),
        out_shape=(jax.ShapeDtypeStruct(o.shape, jnp.float32), jax.ShapeDtypeStruct(w.shape, jnp.float32)),
        in_specs=[spec] * (4 + len(old)),
        out_specs=(spec, spec),
        scratch_shapes=[
            pltpu.VMEM((3, m, 3 * inner), jnp.bfloat16),
            pltpu.VMEM((3, inner, 3 * m), jnp.bfloat16),
        ],
        compiler_params=pltpu.CompilerParams(vmem_limit_bytes=LIMIT),
        cost_estimate=pl.CostEstimate(
            flops=54 * inner * m * n, bytes_accessed=16 * inner * (m + n), transcendentals=m * n
        ),
    )(o, w, gap_o.reshape(m, 1), gap_w.reshape(1, n), *old)


def moved_from(route, by_x, by_z, count_x, count_z):
    out = {}
    for k, target in route.items():
        kx, kz = divmod(k, count_z)
        out[(kx + by_x) % count_x * count_z + (kz + by_z) % count_z] = target
    return out


def body(factors, occ_energy, vir_energy, shifts):
    count_x, count_z = lax.axis_size("kxy"), lax.axis_size("kz")
    odd, after, before = routes(count_x, count_z)
    route_a = {**onto(odd, 0), **onto(after, 1)}
    route_b = {**onto(odd, 1), **onto(before, 0)}
    route_after = onto(after, 1)
    route_before = onto(before, 0)
    cores = {i: i ^ count_z for i in range(count_x * count_z)}
    upper = lax.axis_index("kxy") % 2 == 1

    own = factors[0, 0]
    half = own.shape[-1] // 2
    first, second = own[..., :half], own[..., half:]
    arrived_a = move(first, route_a)
    arrived_b = move(second, route_b)
    rest_after = move(second, route_after)
    rest_before = move(first, route_before)

    def send_energies(by_x, by_z):
        def send(vir):
            return tuple(
                move(vir, moved_from(route, by_x, by_z, count_x, count_z)) for route in (route_a, route_b)
            )

        return send

    span = REACH - 1
    sends = [send_energies(1 + i // span, 1 + i % span) for i in range(span * span)]
    vir_a, vir_b = lax.switch((shifts[0, 0] - 1) * span + shifts[0, 1] - 1, sends, vir_energy[0, 0])
    occ_a = move(occ_energy[0, 0], route_a)
    occ_b = move(occ_energy[0, 0], route_b)
    gap_a = (vir_a[None, :] - occ_a[:, None]).reshape(2, half)
    gap_b = (vir_b[None, :] - occ_b[:, None]).reshape(2, half)
    gap_o = jnp.where(upper, gap_b[::-1], gap_a)
    gap_w = jnp.where(upper, gap_a, gap_b[::-1])

    o_a = jnp.where(upper, arrived_b, arrived_a)
    w_f = jnp.where(upper, arrived_a, arrived_b)
    o_b = move(o_a, cores)
    w_s = jnp.where(upper, rest_after, rest_before)

    to_a, to_f = block(o_a, w_f, gap_o[0], gap_w[0])
    to_b, to_f = block(o_b, w_f, gap_o[1], gap_w[0], old_w=to_f)
    back_after = move_back(to_f, route_after)
    back_before = move_back(to_f, route_before)
    to_b, to_s = block(o_b, w_s, gap_o[1], gap_w[1], old_o=to_b)
    crossed = move(to_b, cores)
    to_a, to_s = block(o_a, w_s, gap_o[0], gap_w[1], to_a, to_s)
    to_a = to_a + crossed
    back_a = move_back(jnp.where(upper, to_s, to_a), route_a)
    back_b = move_back(jnp.where(upper, to_a, to_s), route_b)
    total = jnp.concatenate(
        [
            back_after + jnp.where(upper, back_a, back_b),
            back_before + jnp.where(upper, back_b, back_a),
        ],
        -1,
    )
    return (-total)[None, None]


def solution(mesh):
    placed = (P("kxy", "kz", None, None, None), P("kxy", "kz", None), P("kxy", "kz", None), P())
    return jax.shard_map(
        body,
        mesh=mesh,
        in_specs=placed,
        out_specs=P("kxy", "kz", None, None, None),
        check_vma=False,
    )
```

profile of v0, /device:TPU:20, one launch (start us, length us, event | category | flops | bytes accessed | tf_op | source)
XLA Modules:
  0.0 174.9 jit_solution(5910280680840095249)
XLA Ops:
  0.0 3.9 %fusion = (f32[2,384,512]{2,1,0:T(8,128)}, f32[2,384,512]{2,1,0:T(8,128)}) fusion(f32[2,384,1024]{2,1,0:T(8,128)} %bitcast.28), kind=kLoop, calls=%fused_computation.18 | loop fusion | bytes 6291456 | tf_op jit(solution)/shard_map/slice | solution.py:145
  3.9 4.8 %collective-permute-start.19 = (f32[2,384,512]{2,1,0:T(8,128)}, f32[2,384,512]{2,1,0:T(8,128)S(1)}, u32[]{:S(2)}, u32[]{:S(2)}) collective-permute-start(f32[2,384,512]{2,1,0:T(8,128)} %get-tuple-element.40), channel_id=1, source_target_pairs={{0,25},{1,26},{2,95},{3,24},{4,29},{5,30},{6,91},{7,28},{8,48},{9,... | collective-permute-start | bytes 4718600 | tf_op jit(solution)/shard_map/ppermute | solution.py:42
  8.8 1.2 collective-permute-start.22
  10.0 0.6 fusion.2
  11.8 16.0 %conditional.1 = (f32[128]{0:T(128)}, f32[128]{0:T(128)}) conditional(s32[]{:T(128)} %bitcast.1, f32[128]{0:T(128)S(1)} %bitcast.29, f32[128]{0:T(128)S(1)} %bitcast.30, f32[128]{0:T(128)S(1)} %bitcast.31, f32[128]{0:T(128)S(1)} %bitcast.32, f32[128]{0:T(128)S(1)} %bitcast.33, f32[128]{0:T(128)S(1)} %bitcast.34, ...), branch_computations={%region_0.1_spmd, %region_1.2_spmd, %region_2.3_spmd, %region_3.4_... | conditional | bytes 4192 | solution.py:161
  11.8 2.7 %collective-permute-start.7 = (f32[128]{0:T(128)S(1)}, f32[128]{0:T(128)}, u32[]{:S(2)}, u32[]{:S(2)}) collective-permute-start(f32[128]{0:T(128)S(1)} %param.3), channel_id=1, source_target_pairs={{0,118},{1,115},{2,52},{3,113},{4,114},{5,119},{6,48},{7,117},{8,1... | collective-permute-start | bytes 1544 | tf_op jit(solution)/shard_map/cond/branch_3_fun/ppermute | solution.py:42
  14.6 13.2 %collective-permute-done.7 = f32[128]{0:T(128)} collective-permute-done((f32[128]{0:T(128)S(1)}, f32[128]{0:T(128)}, u32[]{:S(2)}, u32[]{:S(2)}) %collective-permute-start.7) | collective-permute-done | bytes 544 | tf_op jit(solution)/shard_map/cond/branch_3_fun/ppermute | solution.py:42
  27.8 3.4 %collective-permute-start.21 = (f32[8]{0:T(128)S(1)}, f32[8]{0:T(128)S(1)}, u32[]{:S(2)}, u32[]{:S(2)}) collective-permute-start(f32[8]{0:T(128)S(1)} %bitcast.39), channel_id=1, source_target_pairs={{0,3},{1,4},{2,1},{3,2},{4,7},{5,0},{6,5},{7,6},{8,56},{9,125},{10... | collective-permute-start | bytes 104 | tf_op jit(solution)/shard_map/ppermute | solution.py:42
  31.2 3.0 %collective-permute-start.25 = (f32[2,384,512]{2,1,0:T(8,128)}, f32[2,384,512]{2,1,0:T(8,128)}, u32[]{:S(2)}, u32[]{:S(2)}) collective-permute-start(f32[2,384,512]{2,1,0:T(8,128)} %get-tuple-element.40), channel_id=1, source_target_pairs={{0,3},{1,4},{2,1},{3,2},{4,7},{5,0},{6,5},{7,6},{16,19},{17,84},{1... | collective-permute-start | bytes 4718600 | tf_op jit(solution)/shard_map/ppermute | solution.py:42
  34.2 0.7 broadcast_bitcast_fusion.3
  34.9 0.6 broadcast_bitcast_fusion.2
  35.4 15.5 %collective-permute-start.24 = (f32[2,384,512]{2,1,0:T(8,128)}, f32[2,384,512]{2,1,0:T(8,128)}, u32[]{:S(2)}, u32[]{:S(2)}) collective-permute-start(f32[2,384,512]{2,1,0:T(8,128)} %get-tuple-element.41), channel_id=1, source_target_pairs={{0,25},{1,26},{2,95},{3,24},{4,29},{5,30},{6,91},{7,28},{16,41},{1... | collective-permute-start | bytes 4718600 | tf_op jit(solution)/shard_map/ppermute | solution.py:42
  51.2 1.2 copy-done.1
  52.4 2.5 %broadcast_select_fusion.3 = (f32[2,384,512]{2,1,0:T(8,128)S(1)}, f32[2,384,512]{2,1,0:T(8,128)S(1)}) fusion(f32[2,384,512]{2,1,0:T(8,128)} %copy-done.1, f32[2,384,512]{2,1,0:T(8,128)} %collective-permute-done.18, pred[]{:T(512)S(6)} %eq.5), kind=kLoop, calls=%fused_computation.6 | loop fusion | flops 786432 | bytes 6291457 | tf_op jit(solution)/shard_map/jit(_where)/select_n | solution.py:170
  55.1 0.3 rev.4
  55.5 0.9 copy.6.refs_2_
  56.4 11.6 %collective-permute-done.24 = f32[2,384,512]{2,1,0:T(8,128)} collective-permute-done((f32[2,384,512]{2,1,0:T(8,128)}, f32[2,384,512]{2,1,0:T(8,128)}, u32[]{:S(2)}, u32[]{:S(2)}) %collective-permute-start.24) | collective-permute-done | bytes 1572896 | tf_op jit(solution)/shard_map/ppermute | solution.py:42
  68.0 1.8 %broadcast_select_fusion.2.refs_1_ = f32[2,384,512]{2,1,0:T(8,128)S(1)} fusion(f32[2,384,512]{2,1,0:T(8,128)} %collective-permute-done.24, f32[2,384,512]{2,1,0:T(8,128)} %collective-permute-done.25, pred[]{:T(512)S(6)} %eq.5), kind=kLoop, calls=%fused_computation.5 | loop fusion | flops 393216 | bytes 4718593 | tf_op jit(solution)/shard_map/jit(_where)/select_n | solution.py:172
  69.8 6.3 %shard_map.46 = (f32[2,384,512]{2,1,0:T(8,128)S(1)}, f32[2,384,512]{2,1,0:T(8,128)S(1)}) custom-call(f32[2,384,512]{2,1,0:T(8,128)S(1)} %get-tuple-element.39.refs_0_, f32[2,384,512]{2,1,0:T(8,128)S(1)} %get-tuple-element.38.refs_1_, f32[512,1]{1,0:T(8,128)S(1)} %copy.5.refs_2_, f32[1,512]{1,0:T(1,128)S(1)} %get-tuple-element.45.refs_3_), custom_call_target="tpu_custom_call" | custom-call | flops 5435817984 | bytes 6291456 | tf_op jit(solution)/shard_map/pallas_call | solution.py:109
  76.1 7.8 %shard_map.47 = (f32[2,384,512]{2,1,0:T(8,128)S(1)}, f32[2,384,512]{2,1,0:T(8,128)S(1)}) custom-call(f32[2,384,512]{2,1,0:T(8,128)} %collective-permute-done.20.refs_0_, f32[2,384,512]{2,1,0:T(8,128)S(1)} %get-tuple-element.38.refs_1_, f32[512,1]{1,0:T(8,128)S(1)} %copy-done, f32[1,512]{1,0:T(1,128)S(1)} %get-tuple-element.45.refs_3_, ...), custom_call_target="tpu_custom_call" | custom-call | flops 5435817984 | bytes 6291456 | tf_op jit(solution)/shard_map/pallas_call | solution.py:109
  83.9 8.2 %shard_map.48 = (f32[2,384,512]{2,1,0:T(8,128)S(1)}, f32[2,384,512]{2,1,0:T(8,128)S(1)}) custom-call(f32[2,384,512]{2,1,0:T(8,128)} %collective-permute-done.20.refs_0_, f32[2,384,512]{2,1,0:T(8,128)S(1)} %broadcast_select_fusion.2.refs_1_, f32[512,1]{1,0:T(8,128)S(1)} %copy-done, f32[1,512]{1,0:T(1,128)S(1)} %get-tuple-element.44.refs_3_, ...), custom_call_target="tpu_custom_call" | custom-call | flops 5435817984 | bytes 6291456 | tf_op jit(solution)/shard_map/pallas_call | solution.py:109
  92.2 1.9 %collective-permute-start.29 = (f32[2,384,512]{2,1,0:T(8,128)S(1)}, f32[2,384,512]{2,1,0:T(8,128)S(1)}, u32[]{:S(2)}, u32[]{:S(2)}) collective-permute-start(f32[2,384,512]{2,1,0:T(8,128)S(1)} %get-tuple-element.27), channel_id=1, source_target_pairs={{0,5},{1,2},{2,3},{3,0},{4,1},{5,6},{6,7},{7,4},{16,85},{17,82},{1... | collective-permute-start | bytes 4718600 | tf_op jit(solution)/shard_map/ppermute | solution.py:46
  94.1 1.3 collective-permute-start.23
  95.4 6.6 %shard_map.49 = (f32[2,384,512]{2,1,0:T(8,128)S(1)}, f32[2,384,512]{2,1,0:T(8,128)S(1)}) custom-call(f32[2,384,512]{2,1,0:T(8,128)S(1)} %get-tuple-element.39.refs_0_, f32[2,384,512]{2,1,0:T(8,128)S(1)} %broadcast_select_fusion.2.refs_1_, f32[512,1]{1,0:T(8,128)S(1)} %copy.5.refs_2_, f32[1,512]{1,0:T(1,128)S(1)} %get-tuple-element.44.refs_3_, ...), custom_call_target="tpu_custom_call" | custom-call | flops 5435817984 | bytes 6291456 | tf_op jit(solution)/shard_map/pallas_call | solution.py:109
  102.1 0.6 broadcast_select_fusion.1
  102.6 6.1 %collective-permute-start.27 = (f32[2,384,512]{2,1,0:T(8,128)S(1)}, f32[2,384,512]{2,1,0:T(8,128)S(1)}, u32[]{:S(2)}, u32[]{:S(2)}) collective-permute-start(f32[2,384,512]{2,1,0:T(8,128)S(1)} %get-tuple-element.34), channel_id=1, source_target_pairs={{0,24},{1,29},{2,30},{3,27},{4,28},{5,25},{6,26},{7,31},{8,51},{9,... | collective-permute-start | bytes 4718600 | tf_op jit(solution)/shard_map/ppermute | solution.py:46
  108.8 0.9 collective-permute-start.28
  109.7 5.7 %collective-permute-done.29 = f32[2,384,512]{2,1,0:T(8,128)S(1)} collective-permute-done((f32[2,384,512]{2,1,0:T(8,128)S(1)}, f32[2,384,512]{2,1,0:T(8,128)S(1)}, u32[]{:S(2)}, u32[]{:S(2)}) %collective-permute-start.29) | collective-permute-done | bytes 1572896 | tf_op jit(solution)/shard_map/ppermute | solution.py:46
  115.4 11.6 %collective-permute-done.23 = f32[2,384,512]{2,1,0:T(8,128)S(1)} collective-permute-done((f32[2,384,512]{2,1,0:T(8,128)S(1)}, f32[2,384,512]{2,1,0:T(8,128)S(1)}, u32[]{:S(2)}, u32[]{:S(2)}) %collective-permute-start.23) | collective-permute-done | bytes 1572896 | tf_op jit(solution)/shard_map/ppermute | solution.py:46
  127.0 45.1 %collective-permute-done.27 = f32[2,384,512]{2,1,0:T(8,128)S(1)} collective-permute-done((f32[2,384,512]{2,1,0:T(8,128)S(1)}, f32[2,384,512]{2,1,0:T(8,128)S(1)}, u32[]{:S(2)}, u32[]{:S(2)}) %collective-permute-start.27) | collective-permute-done | bytes 1572896 | tf_op jit(solution)/shard_map/ppermute | solution.py:46
  172.1 0.8 add_bitcast_fusion.1
  172.9 2.0 %maximum_negate_fusion = f32[1,1,2,384,1024]{4,3,2,1,0:T(8,128)} fusion(f32[1,1,2,384,512]{4,3,2,1,0:T(8,128)S(1)} %get-tuple-element.37, f32[1,1,2,384,512]{4,3,2,1,0:T(8,128)S(1)} %get-tuple-element.36), kind=kLoop, calls=%fused_computation | loop fusion | flops 1572864 | bytes 6291456 | tf_op jit(solution)/shard_map/neg | solution.py:191
  (31 shorter events, 0.7 us)
Async XLA Ops:
  0.0 8.8 %copy-start.4 = (f32[1,1,8]{2,1,0:T(1,128)S(1)}, f32[1,1,8]{2,1,0:T(1,128)}, u32[]{:S(2)}) copy-start(f32[1,1,8]{2,1,0:T(1,128)} %param.14) | copy-start | bytes 100
  0.0 10.0 %copy-start.2 = (s32[2,2]{1,0:T(2,128)S(1)}, s32[2,2]{1,0:T(2,128)}, u32[]{:S(2)}) copy-start(s32[2,2]{1,0:T(2,128)} %param.16) | copy-start | bytes 52
  0.0 11.8 %copy-start.3 = (f32[1,1,128]{2,1,0:T(1,128)S(1)}, f32[1,1,128]{2,1,0:T(1,128)}, u32[]{:S(2)}) copy-start(f32[1,1,128]{2,1,0:T(1,128)} %param.15) | copy-start | bytes 1540
  3.9 47.3 %collective-permute-start.19 = (f32[2,384,512]{2,1,0:T(8,128)}, f32[2,384,512]{2,1,0:T(8,128)S(1)}, u32[]{:S(2)}, u32[]{:S(2)}) collective-permute-start(f32[2,384,512]{2,1,0:T(8,128)} %get-tuple-element.40), channel_id=1, source_target_pairs={{0,25},{1,26},{2,95},{3,24},{4,29},{5,30},{6,91},{7,28},{8,48},{9,... | collective-permute-start | bytes 4718600 | tf_op jit(solution)/shard_map/ppermute | solution.py:42
  8.8 43.6 %collective-permute-start.18 = (f32[2,384,512]{2,1,0:T(8,128)}, f32[2,384,512]{2,1,0:T(8,128)}, u32[]{:S(2)}, u32[]{:S(2)}) collective-permute-start(f32[2,384,512]{2,1,0:T(8,128)} %get-tuple-element.41), channel_id=1, source_target_pairs={{0,3},{1,4},{2,1},{3,2},{4,7},{5,0},{6,5},{7,6},{8,56},{9,125},{10... | collective-permute-start | bytes 4718600 | tf_op jit(solution)/shard_map/ppermute | solution.py:42
  8.8 42.4 %collective-permute-start.22 = (f32[8]{0:T(128)S(1)}, f32[8]{0:T(128)S(1)}, u32[]{:S(2)}, u32[]{:S(2)}) collective-permute-start(f32[8]{0:T(128)S(1)} %bitcast.38), channel_id=1, source_target_pairs={{0,25},{1,26},{2,95},{3,24},{4,29},{5,30},{6,91},{7,28},{8,48},{9,... | collective-permute-start | bytes 104 | tf_op jit(solution)/shard_map/ppermute | solution.py:42
  11.8 15.9 %collective-permute-start.7 = (f32[128]{0:T(128)S(1)}, f32[128]{0:T(128)}, u32[]{:S(2)}, u32[]{:S(2)}) collective-permute-start(f32[128]{0:T(128)S(1)} %param.3), channel_id=1, source_target_pairs={{0,118},{1,115},{2,52},{3,113},{4,114},{5,119},{6,48},{7,117},{8,1... | collective-permute-start | bytes 1544 | tf_op jit(solution)/shard_map/cond/branch_3_fun/ppermute | solution.py:42
  14.6 13.2 %collective-permute-start.6 = (f32[128]{0:T(128)S(1)}, f32[128]{0:T(128)}, u32[]{:S(2)}, u32[]{:S(2)}) collective-permute-start(f32[128]{0:T(128)S(1)} %param.3), channel_id=1, source_target_pairs={{0,76},{1,73},{2,74},{3,79},{4,72},{5,77},{6,78},{7,75},{8,103},{9... | collective-permute-start | bytes 1544 | tf_op jit(solution)/shard_map/cond/branch_3_fun/ppermute | solution.py:42
  27.8 7.6 %collective-permute-start.21 = (f32[8]{0:T(128)S(1)}, f32[8]{0:T(128)S(1)}, u32[]{:S(2)}, u32[]{:S(2)}) collective-permute-start(f32[8]{0:T(128)S(1)} %bitcast.39), channel_id=1, source_target_pairs={{0,3},{1,4},{2,1},{3,2},{4,7},{5,0},{6,5},{7,6},{8,56},{9,125},{10... | collective-permute-start | bytes 104 | tf_op jit(solution)/shard_map/ppermute | solution.py:42
  31.2 25.2 %collective-permute-start.25 = (f32[2,384,512]{2,1,0:T(8,128)}, f32[2,384,512]{2,1,0:T(8,128)}, u32[]{:S(2)}, u32[]{:S(2)}) collective-permute-start(f32[2,384,512]{2,1,0:T(8,128)} %get-tuple-element.40), channel_id=1, source_target_pairs={{0,3},{1,4},{2,1},{3,2},{4,7},{5,0},{6,5},{7,6},{16,19},{17,84},{1... | collective-permute-start | bytes 4718600 | tf_op jit(solution)/shard_map/ppermute | solution.py:42
  35.4 32.6 %collective-permute-start.24 = (f32[2,384,512]{2,1,0:T(8,128)}, f32[2,384,512]{2,1,0:T(8,128)}, u32[]{:S(2)}, u32[]{:S(2)}) collective-permute-start(f32[2,384,512]{2,1,0:T(8,128)} %get-tuple-element.41), channel_id=1, source_target_pairs={{0,25},{1,26},{2,95},{3,24},{4,29},{5,30},{6,91},{7,28},{16,41},{1... | collective-permute-start | bytes 4718600 | tf_op jit(solution)/shard_map/ppermute | solution.py:42
  51.2 1.2 copy-start.1
  54.9 21.2 %collective-permute-start.20 = (f32[2,384,512]{2,1,0:T(8,128)S(1)}, f32[2,384,512]{2,1,0:T(8,128)}, u32[]{:S(2)}, u32[]{:S(2)}) collective-permute-start(f32[2,384,512]{2,1,0:T(8,128)S(1)} %get-tuple-element.39.refs_0_), channel_id=1, source_target_pairs={{0,8},{1,9},{2,10},{3,11},{4,12},{5,13},{6,14},{7,15},{8,0},{9,1},... | collective-permute-start | bytes 4718600 | tf_op jit(solution)/shard_map/ppermute | solution.py:42
  69.8 6.3 %copy-start = (f32[512,1]{1,0:T(8,128)S(1)}, f32[512,1]{1,0:T(8,128)}, u32[]{:S(2)}) copy-start(f32[512,1]{1,0:T(8,128)} %copy.6.refs_2_) | copy-start | bytes 6148
  92.1 10.0 %collective-permute-start.26 = (f32[2,384,512]{2,1,0:T(8,128)S(1)}, f32[2,384,512]{2,1,0:T(8,128)S(1)}, u32[]{:S(2)}, u32[]{:S(2)}) collective-permute-start(f32[2,384,512]{2,1,0:T(8,128)S(1)} %get-tuple-element.33), channel_id=1, source_target_pairs={{0,8},{1,9},{2,10},{3,11},{4,12},{5,13},{6,14},{7,15},{8,0},{9,1},... | collective-permute-start | bytes 4718600 | tf_op jit(solution)/shard_map/ppermute | solution.py:42
  92.2 23.2 %collective-permute-start.29 = (f32[2,384,512]{2,1,0:T(8,128)S(1)}, f32[2,384,512]{2,1,0:T(8,128)S(1)}, u32[]{:S(2)}, u32[]{:S(2)}) collective-permute-start(f32[2,384,512]{2,1,0:T(8,128)S(1)} %get-tuple-element.27), channel_id=1, source_target_pairs={{0,5},{1,2},{2,3},{3,0},{4,1},{5,6},{6,7},{7,4},{16,85},{17,82},{1... | collective-permute-start | bytes 4718600 | tf_op jit(solution)/shard_map/ppermute | solution.py:46
  94.1 32.9 %collective-permute-start.23 = (f32[2,384,512]{2,1,0:T(8,128)S(1)}, f32[2,384,512]{2,1,0:T(8,128)S(1)}, u32[]{:S(2)}, u32[]{:S(2)}) collective-permute-start(f32[2,384,512]{2,1,0:T(8,128)S(1)} %get-tuple-element.27), channel_id=1, source_target_pairs={{8,51},{9,48},{10,49},{11,54},{12,55},{13,52},{14,53},{15,50},{24,... | collective-permute-start | bytes 4718600 | tf_op jit(solution)/shard_map/ppermute | solution.py:46
  102.6 69.5 %collective-permute-start.27 = (f32[2,384,512]{2,1,0:T(8,128)S(1)}, f32[2,384,512]{2,1,0:T(8,128)S(1)}, u32[]{:S(2)}, u32[]{:S(2)}) collective-permute-start(f32[2,384,512]{2,1,0:T(8,128)S(1)} %get-tuple-element.34), channel_id=1, source_target_pairs={{0,24},{1,29},{2,30},{3,27},{4,28},{5,25},{6,26},{7,31},{8,51},{9,... | collective-permute-start | bytes 4718600 | tf_op jit(solution)/shard_map/ppermute | solution.py:46
  108.8 63.3 %collective-permute-start.28 = (f32[2,384,512]{2,1,0:T(8,128)S(1)}, f32[2,384,512]{2,1,0:T(8,128)S(1)}, u32[]{:S(2)}, u32[]{:S(2)}) collective-permute-start(f32[2,384,512]{2,1,0:T(8,128)S(1)} %get-tuple-element.35), channel_id=1, source_target_pairs={{0,5},{1,2},{2,3},{3,0},{4,1},{5,6},{6,7},{7,4},{8,24},{9,29},{10,... | collective-permute-start | bytes 4718600 | tf_op jit(solution)/shard_map/ppermute | solution.py:46
where the time goes:
time: 175 us
  waiting for transfers between devices  87.3 us (50%)
  starting transfers between devices  41 us (23%)
  Pallas kernels  28.9 us (17%)
  local copies, waits for them, and re-layouts  8.57 us (5%)
  other arithmetic  7.58 us (4%)
    ppermute x4, waiting for transfers between devices, move_back(): return lax.ppermute(x, AXES, sorted(((t, s) for s, t in route.items())))  62.4 us
    ppermute x10, starting transfers between devices, move(): return lax.ppermute(x, AXES, sorted(route.items()))  30.8 us
    pallas_call x4, Pallas kernels, block(): pl.pallas_call(functools.partial(block_kernel, old_o is not None, old_w i...  28.9 us
    ppermute x10, waiting for transfers between devices, move(): return lax.ppermute(x, AXES, sorted(route.items()))  24.9 us
    ppermute x4, starting transfers between devices, move_back(): return lax.ppermute(x, AXES, sorted(((t, s) for s, t in route.items())))  10.2 us
    slice x1, local copies, waits for them, and re-layouts, body(): first, second = (own[..., :half], own[..., half:])  3.92 us
  transfers between devices with their start and end apart: 14, of which 5 were waited for; matrix products, arithmetic and copies ran while one was open for 5% of the time, Pallas kernels for 7%

commit v1 on v0

--- a/solution.py
+++ b/solution.py
@@ -9,7 +9,7 @@
 
 
 REACH = 4
-LIMIT = 26 << 20
+LIMIT = 24 << 20
 AXES = ("kxy", "kz")
 MEET_Z = ((0, 0, 1, 1), (3, 2, 3, 3), (3, 2, 3, 3), (1, 0, 0, 0))
 
@@ -67,13 +67,18 @@
     )
 
 
+def on_upper():
+    return lax.axis_index("kxy") % 2 == 1
+
+
 def block_kernel(has_o, has_w, *refs):
-    o_ref, w_ref, gap_o_ref, gap_w_ref, *refs = refs
+    o_ref, w_ref, gap_o, gap_w, *refs = refs
     old_o = refs.pop(0) if has_o else None
     old_w = refs.pop(0) if has_w else None
     to_o, to_w, tall, flat = refs
+    inner = to_o.shape[1]
+
     a, b = o_ref[0], o_ref[1]
-    inner = a.shape[0]
     for i, x in enumerate((a, b, a + b)):
         flat[i] = left(x, 1)
         high, low = split(x.T)
@@ -84,7 +89,7 @@
     ac = product(tall[0], right(c, 0), 1, 0)
     bd = product(tall[1], right(d, 0), 1, 0)
     both = product(tall[2], right(c - d, 0), 1, 0)
-    inverse = 1.0 / (gap_o_ref[...] + gap_w_ref[...])
+    inverse = 1.0 / (gap_o[...] + gap_w[...])
     p = (ac + bd) * inverse
     q = (both - ac + bd) * inverse
     cp = product(left(c, 1), right(p, 1), 1, 1)
@@ -102,24 +107,23 @@
 
 
 def block(o, w, gap_o, gap_w, old_o=None, old_w=None):
-    inner, m = o.shape[1:]
-    n = w.shape[2]
+    parts, inner, half = o.shape
     old = [x for x in (old_o, old_w) if x is not None]
     spec = pl.BlockSpec(memory_space=pltpu.VMEM)
     return pl.pallas_call(
         functools.partial(block_kernel, old_o is not None, old_w is not None),
-        out_shape=(jax.ShapeDtypeStruct(o.shape, jnp.float32), jax.ShapeDtypeStruct(w.shape, jnp.float32)),
+        out_shape=(jax.ShapeDtypeStruct((parts, inner, half), jnp.float32),) * 2,
         in_specs=[spec] * (4 + len(old)),
         out_specs=(spec, spec),
         scratch_shapes=[
-            pltpu.VMEM((3, m, 3 * inner), jnp.bfloat16),
-            pltpu.VMEM((3, inner, 3 * m), jnp.bfloat16),
+            pltpu.VMEM((3, half, 3 * inner), jnp.bfloat16),
+            pltpu.VMEM((3, inner, 3 * half), jnp.bfloat16),
         ],
         compiler_params=pltpu.CompilerParams(vmem_limit_bytes=LIMIT),
         cost_estimate=pl.CostEstimate(
-            flops=54 * inner * m * n, bytes_accessed=16 * inner * (m + n), transcendentals=m * n
+            flops=54 * inner * half * half, bytes_accessed=32 * inner * half, transcendentals=half * half
         ),
-    )(o, w, gap_o.reshape(m, 1), gap_w.reshape(1, n), *old)
+    )(o, w, gap_o, gap_w, *old)
 
 
 def moved_from(route, by_x, by_z, count_x, count_z):
@@ -128,6 +132,127 @@
         kx, kz = divmod(k, count_z)
         out[(kx + by_x) % count_x * count_z + (kz + by_z) % count_z] = target
     return out
+
+
+def choose_kernel(turned, if_lower, if_upper, first, second, sems):
+    half = first.shape[2]
+    upper = on_upper()
+
+    def copies(source, turned):
+        at = [pl.ds(i * half, half) for i in ((1, 0) if turned else (0, 1))]
+        return (
+            pltpu.make_async_copy(source.at[:, :, at[0]], first, sems.at[0]),
+            pltpu.make_async_copy(source.at[:, :, at[1]], second, sems.at[1]),
+        )
+
+    @pl.when(upper)
+    def _():
+        for copy in copies(if_upper, turned):
+            copy.start()
+
+    @pl.when(jnp.logical_not(upper))
+    def _():
+        for copy in copies(if_lower, False):
+            copy.start()
+
+    for copy in copies(if_lower, False):
+        copy.wait()
+
+
+def choose(if_lower, if_upper, turned):
+    parts, inner, pairs = if_lower.shape
+    spec = pl.BlockSpec(memory_space=pltpu.VMEM)
+    return pl.pallas_call(
+        functools.partial(choose_kernel, turned),
+        out_shape=(jax.ShapeDtypeStruct((parts, inner, pairs // 2), if_lower.dtype),) * 2,
+        in_specs=[pl.BlockSpec(memory_space=pl.ANY)] * 2,
+        out_specs=(spec, spec),
+        scratch_shapes=[pltpu.SemaphoreType.DMA((2,))],
+        compiler_params=pltpu.CompilerParams(vmem_limit_bytes=LIMIT),
+        cost_estimate=pl.CostEstimate(flops=0, bytes_accessed=8 * if_lower.size, transcendentals=0),
+    )(if_lower, if_upper)
+
+
+def gap_kernel(vir_a, vir_b, occ_a, occ_b, first_o, second_o, first_w, second_w):
+    upper = on_upper()
+    occ_o = jnp.where(upper, occ_b[...], occ_a[...])
+    occ_w = jnp.where(upper, occ_a[...], occ_b[...])
+    vir_o = jnp.where(upper, vir_b[...], vir_a[...])
+    vir_w = jnp.where(upper, vir_a[...], vir_b[...])
+    span = vir_o.shape[1]
+    vir_o = jnp.broadcast_to(vir_o, (8, span)).T[:, :1]
+    each = first_o.shape[0] // span
+    for i in range(each):
+        lower_occ, upper_occ = occ_o[:, i : i + 1], occ_o[:, each + i : each + i + 1]
+        at = pl.ds(i * span, span)
+        first_o[at, :] = vir_o - jnp.where(upper, upper_occ, lower_occ)
+        second_o[at, :] = vir_o - jnp.where(upper, lower_occ, upper_occ)
+        first_w[:, at] = vir_w - occ_w[:, i : i + 1]
+        second_w[:, at] = vir_w - occ_w[:, each + i : each + i + 1]
+
+
+def gaps(vir_a, vir_b, occ_a, occ_b):
+    half = vir_a.shape[1] * occ_a.shape[1] // 2
+    spec = pl.BlockSpec(memory_space=pltpu.VMEM)
+    column = jax.ShapeDtypeStruct((half, 1), vir_a.dtype)
+    row = jax.ShapeDtypeStruct((1, half), vir_a.dtype)
+    out = pl.pallas_call(
+        gap_kernel,
+        out_shape=(column, column, row, row),
+        in_specs=[spec] * 4,
+        out_specs=(spec,) * 4,
+        compiler_params=pltpu.CompilerParams(vmem_limit_bytes=LIMIT),
+    )(vir_a, vir_b, occ_a, occ_b)
+    return out[:2], out[2:]
+
+
+def merge_kernel(to_a, met, to_s, for_a, for_b):
+    own = to_a[...] + met[...]
+    other = to_s[...]
+    upper = on_upper()
+    for_a[...] = jnp.where(upper, other, own)
+    for_b[...] = jnp.where(upper, own, other)
+
+
+def merge(to_a, met, to_s):
+    spec = pl.BlockSpec(memory_space=pltpu.VMEM)
+    return pl.pallas_call(
+        merge_kernel,
+        out_shape=(jax.ShapeDtypeStruct(to_a.shape, to_a.dtype),) * 2,
+        in_specs=[spec] * 3,
+        out_specs=(spec, spec),
+        compiler_params=pltpu.CompilerParams(vmem_limit_bytes=LIMIT),
+    )(to_a, met, to_s)
+
+
+def finish_kernel(early, lowered, back_a, back_b, out, held, sems):
+    half = back_a.shape[2]
+    steps = sems.shape[0]
+    rows = back_a.shape[1] // steps
+    upper = on_upper()
+    copies = []
+    for i in range(steps):
+        at = pl.ds(i * rows, rows)
+        a, b = back_a[:, at], back_b[:, at]
+        held[:, at, :half] = -jnp.where(upper, a, early[:, at] + lowered[:, at])
+        held[:, at, half:] = -jnp.where(upper, b, a + b)
+        copies.append(pltpu.make_async_copy(held.at[:, at], out.at[:, at], sems.at[i]))
+        copies[-1].start()
+    for copy in copies:
+        copy.wait()
+
+
+def finish(*backs):
+    parts, inner, half = backs[0].shape
+    shape = (parts, inner, 2 * half)
+    return pl.pallas_call(
+        finish_kernel,
+        out_shape=jax.ShapeDtypeStruct(shape, backs[0].dtype),
+        in_specs=[pl.BlockSpec(memory_space=pltpu.VMEM)] * 4,
+        out_specs=pl.BlockSpec(memory_space=pl.ANY),
+        scratch_shapes=[pltpu.VMEM(shape, backs[0].dtype), pltpu.SemaphoreType.DMA((6,))],
+        compiler_params=pltpu.CompilerParams(vmem_limit_bytes=LIMIT),
+    )(*backs)
 
 
 def body(factors, occ_energy, vir_energy, shifts):
@@ -138,15 +263,16 @@
     route_after = onto(after, 1)
     route_before = onto(before, 0)
     cores = {i: i ^ count_z for i in range(count_x * count_z)}
-    upper = lax.axis_index("kxy") % 2 == 1
+    route_early = {t: s for s, t in route_after.items()} | {t: s ^ count_z for s, t in route_before.items()}
+    downward = {s: t for s, t in cores.items() if s > t}
+    upward = {s: t for s, t in cores.items() if s < t}
 
     own = factors[0, 0]
-    half = own.shape[-1] // 2
-    first, second = own[..., :half], own[..., half:]
-    arrived_a = move(first, route_a)
-    arrived_b = move(second, route_b)
-    rest_after = move(second, route_after)
-    rest_before = move(first, route_before)
+    arrived_a = move(own, route_a)
+    arrived_b = move(own, route_before)
+
+    occ_a = move(occ_energy[0], route_a)
+    occ_b = move(occ_energy[0], route_b)
 
     def send_energies(by_x, by_z):
         def send(vir):
@@ -158,37 +284,24 @@
 
     span = REACH - 1
     sends = [send_energies(1 + i // span, 1 + i % span) for i in range(span * span)]
-    vir_a, vir_b = lax.switch((shifts[0, 0] - 1) * span + shifts[0, 1] - 1, sends, vir_energy[0, 0])
-    occ_a = move(occ_energy[0, 0], route_a)
-    occ_b = move(occ_energy[0, 0], route_b)
-    gap_a = (vir_a[None, :] - occ_a[:, None]).reshape(2, half)
-    gap_b = (vir_b[None, :] - occ_b[:, None]).reshape(2, half)
-    gap_o = jnp.where(upper, gap_b[::-1], gap_a)
-    gap_w = jnp.where(upper, gap_a, gap_b[::-1])
-
-    o_a = jnp.where(upper, arrived_b, arrived_a)
-    w_f = jnp.where(upper, arrived_a, arrived_b)
-    o_b = move(o_a, cores)
-    w_s = jnp.where(upper, rest_after, rest_before)
-
-    to_a, to_f = block(o_a, w_f, gap_o[0], gap_w[0])
-    to_b, to_f = block(o_b, w_f, gap_o[1], gap_w[0], old_w=to_f)
-    back_after = move_back(to_f, route_after)
-    back_before = move_back(to_f, route_before)
-    to_b, to_s = block(o_b, w_s, gap_o[1], gap_w[1], old_o=to_b)
-    crossed = move(to_b, cores)
-    to_a, to_s = block(o_a, w_s, gap_o[0], gap_w[1], to_a, to_s)
-    to_a = to_a + crossed
-    back_a = move_back(jnp.where(upper, to_s, to_a), route_a)
-    back_b = move_back(jnp.where(upper, to_a, to_s), route_b)
-    total = jnp.concatenate(
-        [
-            back_after + jnp.where(upper, back_a, back_b),
-            back_before + jnp.where(upper, back_b, back_a),
-        ],
-        -1,
-    )
-    return (-total)[None, None]
+    vir_a, vir_b = lax.switch((shifts[0, 0] - 1) * span + shifts[0, 1] - 1, sends, vir_energy[0])
+    arrived_a, vir_a, vir_b = lax.optimization_barrier((arrived_a, vir_a, vir_b))
+    crossed = move(arrived_a, upward)
+    w = choose(arrived_b, arrived_a, False)
+    gap_o, gap_w = gaps(vir_a, vir_b, occ_a, occ_b)
+    o = choose(arrived_a, crossed, True)
+
+    to_a, to_f = block(o[0], w[0], gap_o[0], gap_w[0])
+    to_b, to_f = block(o[1], w[0], gap_o[1], gap_w[0], old_w=to_f)
+    back_early = move(to_f, route_early)
+    to_b, to_s = block(o[1], w[1], gap_o[1], gap_w[1], old_o=to_b)
+    met = move(to_b, cores)
+    to_a, to_s = block(o[0], w[1], gap_o[0], gap_w[1], to_a, to_s)
+    for_a, for_b = merge(to_a, met, to_s)
+    back_a = move_back(for_a, route_a)
+    back_b = move_back(for_b, route_b)
+    lowered = move(back_early, downward)
+    return finish(back_early, lowered, back_a, back_b)[None, None]
 
 
 def solution(mesh):

time: 175 us -> 152 us (0.87)
  the two profiles are of different devices: /device:TPU:20 before, /device:TPU:3 now
where the time goes in v1:
time: 152 us; the launch traced here: 151 us
  waiting for transfers between devices  86.6 us (57%)
  starting transfers between devices  31.4 us (21%)
  Pallas kernels  30.7 us (20%)
    ppermute x10, waiting for transfers between devices, move(): return lax.ppermute(x, AXES, sorted(route.items()))  46.4 us
    ppermute x2, waiting for transfers between devices, move_back(): return lax.ppermute(x, AXES, sorted(((t, s) for s, t in route.items())))  40.2 us
    ppermute x10, starting transfers between devices, move(): return lax.ppermute(x, AXES, sorted(route.items()))  27.3 us
    pallas_call x4, Pallas kernels, block(): pl.pallas_call(functools.partial(block_kernel, old_o is not None, old_w i...  26.3 us
    ppermute x2, starting transfers between devices, move_back(): return lax.ppermute(x, AXES, sorted(((t, s) for s, t in route.items())))  4.05 us
  transfers between devices with their start and end apart: 12, of which 6 were waited for; matrix products, arithmetic and copies ran while one was open for 1% of the time, Pallas kernels for 6%

profile of v1, /device:TPU:3, one launch (start us, length us, event | category | flops | bytes accessed | tf_op | source)
XLA Modules:
  0.0 151.5 jit_solution(2111512516056458586)
XLA Ops:
  0.0 6.8 %collective-permute-start.18 = (f32[2,384,1024]{2,1,0:T(8,128)}, f32[2,384,1024]{2,1,0:T(8,128)S(1)}, u32[]{:S(2)}, u32[]{:S(2)}) collective-permute-start(f32[2,384,1024]{2,1,0:T(8,128)} %bitcast.5), channel_id=1, source_target_pairs={{0,25},{1,26},{2,95},{3,24},{4,29},{5,30},{6,91},{7,28},{8,48},{9,... | collective-permute-start | bytes 9437192 | tf_op jit(solution)/shard_map/ppermute | solution.py:42
  6.8 2.3 %collective-permute-start.20 = (f32[2,384,1024]{2,1,0:T(8,128)}, f32[2,384,1024]{2,1,0:T(8,128)}, u32[]{:S(2)}, u32[]{:S(2)}) collective-permute-start(f32[2,384,1024]{2,1,0:T(8,128)} %bitcast.6), channel_id=1, source_target_pairs={{0,3},{1,4},{2,1},{3,2},{4,7},{5,0},{6,5},{7,6},{16,19},{17,84},{1... | collective-permute-start | bytes 9437192 | tf_op jit(solution)/shard_map/ppermute | solution.py:42
  9.1 1.3 fusion
  11.6 7.4 %conditional.1 = (f32[1,128]{1,0:T(1,128)}, f32[1,128]{1,0:T(1,128)}) conditional(s32[]{:T(128)} %bitcast.1, f32[1,128]{1,0:T(1,128)} %bitcast.7, f32[1,128]{1,0:T(1,128)} %bitcast.8, f32[1,128]{1,0:T(1,128)} %bitcast.9, f32[1,128]{1,0:T(1,128)} %bitcast.10, f32[1,128]{1,0:T(1,128)} %bitcast.11, ...), branch_computations={%region_0.0_spmd, %region_1.0_spmd, %region_2.0_spmd, %region_3.0_... | conditional | bytes 4192 | solution.py:287
  11.6 0.1 collective-permute-start.7
  11.7 5.0 %collective-permute-start.6 = (f32[1,128]{1,0:T(1,128)}, f32[1,128]{1,0:T(1,128)}, u32[]{:S(2)}, u32[]{:S(2)}) collective-permute-start(f32[1,128]{1,0:T(1,128)} %param.3), channel_id=1, source_target_pairs={{0,76},{1,73},{2,74},{3,79},{4,72},{5,77},{6,78},{7,75},{8,103},{9... | collective-permute-start | bytes 1544 | tf_op jit(solution)/shard_map/cond/branch_3_fun/ppermute | solution.py:42
  16.7 2.3 %collective-permute-done.7 = f32[1,128]{1,0:T(1,128)} collective-permute-done((f32[1,128]{1,0:T(1,128)}, f32[1,128]{1,0:T(1,128)}, u32[]{:S(2)}, u32[]{:S(2)}) %collective-permute-start.7) | collective-permute-done | bytes 544 | tf_op jit(solution)/shard_map/cond/branch_3_fun/ppermute | solution.py:42
  19.0 0.0 collective-permute-done.6
  19.0 22.3 %collective-permute-done.18.if_lower.if_upper = f32[2,384,1024]{2,1,0:T(8,128)S(1)} collective-permute-done((f32[2,384,1024]{2,1,0:T(8,128)}, f32[2,384,1024]{2,1,0:T(8,128)S(1)}, u32[]{:S(2)}, u32[]{:S(2)}) %collective-permute-start.18) | collective-permute-done | bytes 3145760 | tf_op jit(solution)/shard_map/ppermute | solution.py:42
  41.3 1.3 collective-permute-start.19
  42.6 4.0 %collective-permute-start.22 = (f32[1,8]{1,0:T(1,128)}, f32[1,8]{1,0:T(1,128)S(1)}, u32[]{:S(2)}, u32[]{:S(2)}) collective-permute-start(f32[1,8]{1,0:T(1,128)} %bitcast.16), channel_id=1, source_target_pairs={{0,3},{1,4},{2,1},{3,2},{4,7},{5,0},{6,5},{7,6},{8,56},{9,125},{10... | collective-permute-start | bytes 104 | tf_op jit(solution)/shard_map/ppermute | solution.py:42
  46.6 3.7 %collective-permute-start.21 = (f32[1,8]{1,0:T(1,128)}, f32[1,8]{1,0:T(1,128)S(1)}, u32[]{:S(2)}, u32[]{:S(2)}) collective-permute-start(f32[1,8]{1,0:T(1,128)} %bitcast.17), channel_id=1, source_target_pairs={{0,25},{1,26},{2,95},{3,24},{4,29},{5,30},{6,91},{7,28},{8,48},{9,... | collective-permute-start | bytes 104 | tf_op jit(solution)/shard_map/ppermute | solution.py:42
  50.3 0.0 collective-permute-done.20.if_lower
  50.3 0.5 shard_map.47
  50.8 0.0 collective-permute-done.22.occ_b
  50.8 3.0 %collective-permute-done.21.occ_a = f32[1,8]{1,0:T(1,128)S(1)} collective-permute-done((f32[1,8]{1,0:T(1,128)}, f32[1,8]{1,0:T(1,128)S(1)}, u32[]{:S(2)}, u32[]{:S(2)}) %collective-permute-start.21) | collective-permute-done | bytes 64 | tf_op jit(solution)/shard_map/ppermute | solution.py:42
  53.8 0.8 shard_map.48
  54.6 0.8 shard_map.46
  55.4 6.4 %shard_map.49 = (f32[2,384,512]{2,1,0:T(8,128)S(1)}, f32[2,384,512]{2,1,0:T(8,128)S(1)}) custom-call(f32[2,384,512]{2,1,0:T(8,128)S(1)} %get-tuple-element.46.refs_0_, f32[2,384,512]{2,1,0:T(8,128)S(1)} %get-tuple-element.41.refs_1_, f32[512,1]{1,0:T(8,128)S(1)} %get-tuple-element.47.refs_2_, f32[1,512]{1,0:T(1,128)S(1)} %get-tuple-element.45.refs_3_), custom_call_target="tpu_custom_call" | custom-call | flops 5435817984 | bytes 6291456 | tf_op jit(solution)/shard_map/pallas_call | solution.py:113
  61.8 6.5 %shard_map.50 = (f32[2,384,512]{2,1,0:T(8,128)S(1)}, f32[2,384,512]{2,1,0:T(8,128)S(1)}) custom-call(f32[2,384,512]{2,1,0:T(8,128)S(1)} %get-tuple-element.40.refs_0_, f32[2,384,512]{2,1,0:T(8,128)S(1)} %get-tuple-element.41.refs_1_, f32[512,1]{1,0:T(8,128)S(1)} %get-tuple-element.44.refs_2_, f32[1,512]{1,0:T(1,128)S(1)} %get-tuple-element.45.refs_3_, ...), custom_call_target="tpu_custom_call" | custom-call | flops 5435817984 | bytes 6291456 | tf_op jit(solution)/shard_map/pallas_call | solution.py:113
  68.4 6.8 %shard_map.51 = (f32[2,384,512]{2,1,0:T(8,128)S(1)}, f32[2,384,512]{2,1,0:T(8,128)S(1)}) custom-call(f32[2,384,512]{2,1,0:T(8,128)S(1)} %get-tuple-element.40.refs_0_, f32[2,384,512]{2,1,0:T(8,128)S(1)} %get-tuple-element.50.refs_1_, f32[512,1]{1,0:T(8,128)S(1)} %get-tuple-element.44.refs_2_, f32[1,512]{1,0:T(1,128)S(1)} %get-tuple-element.51.refs_3_, ...), custom_call_target="tpu_custom_call" | custom-call | flops 5435817984 | bytes 6291456 | tf_op jit(solution)/shard_map/pallas_call | solution.py:113
  75.1 1.6 %collective-permute-start.25 = (f32[2,384,512]{2,1,0:T(8,128)S(1)}, f32[2,384,512]{2,1,0:T(8,128)S(1)}, u32[]{:S(2)}, u32[]{:S(2)}) collective-permute-start(f32[2,384,512]{2,1,0:T(8,128)S(1)} %get-tuple-element.56), channel_id=1, source_target_pairs={{0,8},{1,9},{2,10},{3,11},{4,12},{5,13},{6,14},{7,15},{8,0},{9,1},... | collective-permute-start | bytes 4718600 | tf_op jit(solution)/shard_map/ppermute | solution.py:42
  76.7 1.3 collective-permute-start.23
  78.0 6.6 %shard_map.52 = (f32[2,384,512]{2,1,0:T(8,128)S(1)}, f32[2,384,512]{2,1,0:T(8,128)S(1)}) custom-call(f32[2,384,512]{2,1,0:T(8,128)S(1)} %get-tuple-element.46.refs_0_, f32[2,384,512]{2,1,0:T(8,128)S(1)} %get-tuple-element.50.refs_1_, f32[512,1]{1,0:T(8,128)S(1)} %get-tuple-element.47.refs_2_, f32[1,512]{1,0:T(1,128)S(1)} %get-tuple-element.51.refs_3_, ...), custom_call_target="tpu_custom_call" | custom-call | flops 5435817984 | bytes 6291456 | tf_op jit(solution)/shard_map/pallas_call | solution.py:113
  84.7 0.4 shard_map.53
  85.1 1.6 %collective-permute-start.26 = (f32[2,384,512]{2,1,0:T(8,128)S(1)}, f32[2,384,512]{2,1,0:T(8,128)S(1)}, u32[]{:S(2)}, u32[]{:S(2)}) collective-permute-start(f32[2,384,512]{2,1,0:T(8,128)S(1)} %get-tuple-element.58), channel_id=1, source_target_pairs={{0,24},{1,29},{2,30},{3,27},{4,28},{5,25},{6,26},{7,31},{8,51},{9,... | collective-permute-start | bytes 4718600 | tf_op jit(solution)/shard_map/ppermute | solution.py:46
  86.7 2.5 %collective-permute-start.27 = (f32[2,384,512]{2,1,0:T(8,128)S(1)}, f32[2,384,512]{2,1,0:T(8,128)S(1)}, u32[]{:S(2)}, u32[]{:S(2)}) collective-permute-start(f32[2,384,512]{2,1,0:T(8,128)S(1)} %get-tuple-element.59), channel_id=1, source_target_pairs={{0,5},{1,2},{2,3},{3,0},{4,1},{5,6},{6,7},{7,4},{8,24},{9,29},{10,... | collective-permute-start | bytes 4718600 | tf_op jit(solution)/shard_map/ppermute | solution.py:46
  89.2 18.8 %collective-permute-done.23.early = f32[2,384,512]{2,1,0:T(8,128)S(1)} collective-permute-done((f32[2,384,512]{2,1,0:T(8,128)S(1)}, f32[2,384,512]{2,1,0:T(8,128)S(1)}, u32[]{:S(2)}, u32[]{:S(2)}) %collective-permute-start.23) | collective-permute-done | bytes 1572896 | tf_op jit(solution)/shard_map/ppermute | solution.py:42
  107.9 1.4 collective-permute-start.24
  109.3 39.2 %collective-permute-done.26.back_a = f32[2,384,512]{2,1,0:T(8,128)S(1)} collective-permute-done((f32[2,384,512]{2,1,0:T(8,128)S(1)}, f32[2,384,512]{2,1,0:T(8,128)S(1)}, u32[]{:S(2)}, u32[]{:S(2)}) %collective-permute-start.26) | collective-permute-done | bytes 1572896 | tf_op jit(solution)/shard_map/ppermute | solution.py:46
  148.6 0.9 collective-permute-done.27.back_b
  149.5 1.8 %shard_map.54 = f32[2,384,1024]{2,1,0:T(8,128)} custom-call(f32[2,384,512]{2,1,0:T(8,128)S(1)} %collective-permute-done.23.early, f32[2,384,512]{2,1,0:T(8,128)S(1)} %collective-permute-done.24.lowered, f32[2,384,512]{2,1,0:T(8,128)S(1)} %collective-permute-done.26.back_a, f32[2,384,512]{2,1,0:T(8,128)S(1)} %collective-permute-done.27.back_b), custom_call_target="tpu_custom_call" | custom-call | tf_op jit(solution)/shard_map/pallas_call | solution.py:248
  (3 shorter events, 0.0 us)
Async XLA Ops:
  0.0 41.3 %collective-permute-start.18 = (f32[2,384,1024]{2,1,0:T(8,128)}, f32[2,384,1024]{2,1,0:T(8,128)S(1)}, u32[]{:S(2)}, u32[]{:S(2)}) collective-permute-start(f32[2,384,1024]{2,1,0:T(8,128)} %bitcast.5), channel_id=1, source_target_pairs={{0,25},{1,26},{2,95},{3,24},{4,29},{5,30},{6,91},{7,28},{8,48},{9,... | collective-permute-start | bytes 9437192 | tf_op jit(solution)/shard_map/ppermute | solution.py:42
  6.8 43.5 %collective-permute-start.20 = (f32[2,384,1024]{2,1,0:T(8,128)}, f32[2,384,1024]{2,1,0:T(8,128)}, u32[]{:S(2)}, u32[]{:S(2)}) collective-permute-start(f32[2,384,1024]{2,1,0:T(8,128)} %bitcast.6), channel_id=1, source_target_pairs={{0,3},{1,4},{2,1},{3,2},{4,7},{5,0},{6,5},{7,6},{16,19},{17,84},{1... | collective-permute-start | bytes 9437192 | tf_op jit(solution)/shard_map/ppermute | solution.py:42
  11.6 7.4 %collective-permute-start.7 = (f32[1,128]{1,0:T(1,128)}, f32[1,128]{1,0:T(1,128)}, u32[]{:S(2)}, u32[]{:S(2)}) collective-permute-start(f32[1,128]{1,0:T(1,128)} %param.3), channel_id=1, source_target_pairs={{0,118},{1,115},{2,52},{3,113},{4,114},{5,119},{6,48},{7,117},{8,1... | collective-permute-start | bytes 1544 | tf_op jit(solution)/shard_map/cond/branch_3_fun/ppermute | solution.py:42
  11.7 7.3 %collective-permute-start.6 = (f32[1,128]{1,0:T(1,128)}, f32[1,128]{1,0:T(1,128)}, u32[]{:S(2)}, u32[]{:S(2)}) collective-permute-start(f32[1,128]{1,0:T(1,128)} %param.3), channel_id=1, source_target_pairs={{0,76},{1,73},{2,74},{3,79},{4,72},{5,77},{6,78},{7,75},{8,103},{9... | collective-permute-start | bytes 1544 | tf_op jit(solution)/shard_map/cond/branch_3_fun/ppermute | solution.py:42
  41.3 13.3 %collective-permute-start.19 = (f32[2,384,1024]{2,1,0:T(8,128)S(1)}, f32[2,384,1024]{2,1,0:T(8,128)S(1)}, u32[]{:S(2)}, u32[]{:S(2)}) collective-permute-start(f32[2,384,1024]{2,1,0:T(8,128)S(1)} %collective-permute-done.18.if_lower.if_upper), channel_id=1, source_target_pairs={{0,8},{1,9},{2,10},{3,11},{4,12},{5,13},{6,14},{7,15},{16,24},{17,... | collective-permute-start | bytes 9437192 | tf_op jit(solution)/shard_map/ppermute | solution.py:42
  42.6 8.2 %collective-permute-start.22 = (f32[1,8]{1,0:T(1,128)}, f32[1,8]{1,0:T(1,128)S(1)}, u32[]{:S(2)}, u32[]{:S(2)}) collective-permute-start(f32[1,8]{1,0:T(1,128)} %bitcast.16), channel_id=1, source_target_pairs={{0,3},{1,4},{2,1},{3,2},{4,7},{5,0},{6,5},{7,6},{8,56},{9,125},{10... | collective-permute-start | bytes 104 | tf_op jit(solution)/shard_map/ppermute | solution.py:42
  46.6 7.2 %collective-permute-start.21 = (f32[1,8]{1,0:T(1,128)}, f32[1,8]{1,0:T(1,128)S(1)}, u32[]{:S(2)}, u32[]{:S(2)}) collective-permute-start(f32[1,8]{1,0:T(1,128)} %bitcast.17), channel_id=1, source_target_pairs={{0,25},{1,26},{2,95},{3,24},{4,29},{5,30},{6,91},{7,28},{8,48},{9,... | collective-permute-start | bytes 104 | tf_op jit(solution)/shard_map/ppermute | solution.py:42
  75.1 9.5 %collective-permute-start.25 = (f32[2,384,512]{2,1,0:T(8,128)S(1)}, f32[2,384,512]{2,1,0:T(8,128)S(1)}, u32[]{:S(2)}, u32[]{:S(2)}) collective-permute-start(f32[2,384,512]{2,1,0:T(8,128)S(1)} %get-tuple-element.56), channel_id=1, source_target_pairs={{0,8},{1,9},{2,10},{3,11},{4,12},{5,13},{6,14},{7,15},{8,0},{9,1},... | collective-permute-start | bytes 4718600 | tf_op jit(solution)/shard_map/ppermute | solution.py:42
  76.7 31.2 %collective-permute-start.23 = (f32[2,384,512]{2,1,0:T(8,128)S(1)}, f32[2,384,512]{2,1,0:T(8,128)S(1)}, u32[]{:S(2)}, u32[]{:S(2)}) collective-permute-start(f32[2,384,512]{2,1,0:T(8,128)S(1)} %get-tuple-element.49), channel_id=1, source_target_pairs={{0,13},{1,10},{2,11},{3,8},{4,9},{5,14},{6,15},{7,12},{8,51},{9,48... | collective-permute-start | bytes 4718600 | tf_op jit(solution)/shard_map/ppermute | solution.py:42
  85.1 63.5 %collective-permute-start.26 = (f32[2,384,512]{2,1,0:T(8,128)S(1)}, f32[2,384,512]{2,1,0:T(8,128)S(1)}, u32[]{:S(2)}, u32[]{:S(2)}) collective-permute-start(f32[2,384,512]{2,1,0:T(8,128)S(1)} %get-tuple-element.58), channel_id=1, source_target_pairs={{0,24},{1,29},{2,30},{3,27},{4,28},{5,25},{6,26},{7,31},{8,51},{9,... | collective-permute-start | bytes 4718600 | tf_op jit(solution)/shard_map/ppermute | solution.py:46
  86.7 62.8 %collective-permute-start.27 = (f32[2,384,512]{2,1,0:T(8,128)S(1)}, f32[2,384,512]{2,1,0:T(8,128)S(1)}, u32[]{:S(2)}, u32[]{:S(2)}) collective-permute-start(f32[2,384,512]{2,1,0:T(8,128)S(1)} %get-tuple-element.59), channel_id=1, source_target_pairs={{0,5},{1,2},{2,3},{3,0},{4,1},{5,6},{6,7},{7,4},{8,24},{9,29},{10,... | collective-permute-start | bytes 4718600 | tf_op jit(solution)/shard_map/ppermute | solution.py:46
  107.9 41.6 %collective-permute-start.24 = (f32[2,384,512]{2,1,0:T(8,128)S(1)}, f32[2,384,512]{2,1,0:T(8,128)S(1)}, u32[]{:S(2)}, u32[]{:S(2)}) collective-permute-start(f32[2,384,512]{2,1,0:T(8,128)S(1)} %collective-permute-done.23.early), channel_id=1, source_target_pairs={{8,0},{9,1},{10,2},{11,3},{12,4},{13,5},{14,6},{15,7},{24,16},{25,... | collective-permute-start | bytes 4718600 | tf_op jit(solution)/shard_map/ppermute | solution.py:42

commit v2 on v1

--- a/solution.py
+++ b/solution.py
@@ -12,6 +12,10 @@
 LIMIT = 24 << 20
 AXES = ("kxy", "kz")
 MEET_Z = ((0, 0, 1, 1), (3, 2, 3, 3), (3, 2, 3, 3), (1, 0, 0, 0))
+AROUND_AFTER = {(1, 3): (1, 3, 1), (3, 1): (3, 1, 1), (3, 2): (3, 2, 1), (3, 3): (3, 3, 1)}
+AROUND_BEFORE = {(0, 0): (0, 0, 0), (0, 1): (0, 1, 0), (0, 2): (0, 2, 0), (0, 3): (0, 3, 0)}
+PARTED_AFTER = {(3, 0): (3, 3, 0)}
+PARTED_BEFORE = {(1, 1): (0, 1, 1)}
 
 
 def coordinates(kx, kz):
@@ -32,6 +36,18 @@
             after[(kx + 3) % count_x * count_z + (kz + 3) % count_z] = meet
             before[(kx - 3) % count_x * count_z + (kz - 3) % count_z] = meet
     return odd, after, before
+
+
+def around(meets, core, table, count_z):
+    first, second, homes = {}, {}, set()
+    for home, (x, y, z) in meets.items():
+        if (x, y % 4) in table:
+            column_x, column_y, column_core = table[x, y % 4]
+            middle = device(column_x, column_y, coordinates(*divmod(home, count_z))[2], column_core)
+            first[device(x, y, z, core)] = middle
+            second[middle] = home
+            homes.add(home)
+    return first, second, homes
 
 
 def onto(meets, core):
@@ -206,26 +222,30 @@
     return out[:2], out[2:]
 
 
-def merge_kernel(to_a, met, to_s, for_a, for_b):
+def merge_kernel(to_a, met, to_s, for_a, for_b, for_re, for_im):
     own = to_a[...] + met[...]
     other = to_s[...]
     upper = on_upper()
     for_a[...] = jnp.where(upper, other, own)
     for_b[...] = jnp.where(upper, own, other)
+    for_re[...] = other[0]
+    for_im[...] = other[1]
 
 
 def merge(to_a, met, to_s):
     spec = pl.BlockSpec(memory_space=pltpu.VMEM)
+    whole = jax.ShapeDtypeStruct(to_a.shape, to_a.dtype)
+    part = jax.ShapeDtypeStruct(to_a.shape[1:], to_a.dtype)
     return pl.pallas_call(
         merge_kernel,
-        out_shape=(jax.ShapeDtypeStruct(to_a.shape, to_a.dtype),) * 2,
+        out_shape=(whole, whole, part, part),
         in_specs=[spec] * 3,
-        out_specs=(spec, spec),
+        out_specs=(spec,) * 4,
         compiler_params=pltpu.CompilerParams(vmem_limit_bytes=LIMIT),
     )(to_a, met, to_s)
 
 
-def finish_kernel(early, lowered, back_a, back_b, out, held, sems):
+def finish_kernel(early, lowered, back_a, back_b, hop, back_re, back_im, out, held, sems):
     half = back_a.shape[2]
     steps = sems.shape[0]
     rows = back_a.shape[1] // steps
@@ -235,7 +255,9 @@
         at = pl.ds(i * rows, rows)
         a, b = back_a[:, at], back_b[:, at]
         held[:, at, :half] = -jnp.where(upper, a, early[:, at] + lowered[:, at])
-        held[:, at, half:] = -jnp.where(upper, b, a + b)
+        even = a + b + hop[:, at]
+        held[0, at, half:] = -jnp.where(upper, b[0], even[0] + back_re[at])
+        held[1, at, half:] = -jnp.where(upper, b[1], even[1] + back_im[at])
         copies.append(pltpu.make_async_copy(held.at[:, at], out.at[:, at], sems.at[i]))
         copies[-1].start()
     for copy in copies:
@@ -248,7 +270,7 @@
     return pl.pallas_call(
         finish_kernel,
         out_shape=jax.ShapeDtypeStruct(shape, backs[0].dtype),
-        in_specs=[pl.BlockSpec(memory_space=pltpu.VMEM)] * 4,
+        in_specs=[pl.BlockSpec(memory_space=pltpu.VMEM)] * 7,
         out_specs=pl.BlockSpec(memory_space=pl.ANY),
         scratch_shapes=[pltpu.VMEM(shape, backs[0].dtype), pltpu.SemaphoreType.DMA((6,))],
         compiler_params=pltpu.CompilerParams(vmem_limit_bytes=LIMIT),
@@ -264,6 +286,18 @@
     route_before = onto(before, 0)
     cores = {i: i ^ count_z for i in range(count_x * count_z)}
     route_early = {t: s for s, t in route_after.items()} | {t: s ^ count_z for s, t in route_before.items()}
+    first_after, second_after, homes_after = around(after, 1, AROUND_AFTER, count_z)
+    first_before, second_before, homes_before = around(before, 0, AROUND_BEFORE, count_z)
+    first_hop = {**first_after, **first_before}
+    second_hop = {**second_after, **second_before}
+    part_after, leave_after, parted_after = around(after, 1, PARTED_AFTER, count_z)
+    part_before, leave_before, parted_before = around(before, 0, PARTED_BEFORE, count_z)
+    part_hop = {**part_after, **part_before}
+    leave_hop = {**leave_after, **leave_before}
+    straight = {route_after[s]: s for s in parted_after} | {route_before[s]: s for s in parted_before}
+    not_a, not_b = homes_after | parted_after, homes_before | parted_before
+    late_a = {**onto(odd, 0), **{s: t for s, t in route_after.items() if s not in not_a}}
+    late_b = {**onto(odd, 1), **{s: t for s, t in route_before.items() if s not in not_b}}
     downward = {s: t for s, t in cores.items() if s > t}
     upward = {s: t for s, t in cores.items() if s < t}
 
@@ -297,11 +331,16 @@
     to_b, to_s = block(o[1], w[1], gap_o[1], gap_w[1], old_o=to_b)
     met = move(to_b, cores)
     to_a, to_s = block(o[0], w[1], gap_o[0], gap_w[1], to_a, to_s)
-    for_a, for_b = merge(to_a, met, to_s)
-    back_a = move_back(for_a, route_a)
-    back_b = move_back(for_b, route_b)
+    middle = move(to_s, first_hop)
+    for_a, for_b, for_re, for_im = merge(to_a, met, to_s)
+    part = move(for_im, part_hop)
+    back_a = move_back(for_a, late_a)
+    back_b = move_back(for_b, late_b)
+    back_re = move(for_re, straight)
     lowered = move(back_early, downward)
-    return finish(back_early, lowered, back_a, back_b)[None, None]
+    hop = move(middle, second_hop)
+    back_im = move(part, leave_hop)
+    return finish(back_early, lowered, back_a, back_b, hop, back_re, back_im)[None, None]
 
 
 def solution(mesh):

time: 152 us -> 153 us (level)
  the two profiles are of different devices: /device:TPU:3 before, /device:TPU:12 now
where the time goes in v2:
time: 153 us; the launch traced here: 152 us
  waiting for transfers between devices  90.8 us (59%)
  Pallas kernels  31.9 us (21%)
  starting transfers between devices  26.5 us (17%)
  between operations  1.62 us (1%)
    ppermute x15, waiting for transfers between devices, move(): return lax.ppermute(x, AXES, sorted(route.items()))  90.8 us
    pallas_call x4, Pallas kernels, block(): pl.pallas_call(functools.partial(block_kernel, old_o is not None, old_w i...  26.3 us
    ppermute x15, starting transfers between devices, move(): return lax.ppermute(x, AXES, sorted(route.items()))  23.8 us
  transfers between devices with their start and end apart: 17, of which 6 were waited for; matrix products, arithmetic and copies ran while one was open for 1% of the time, Pallas kernels for 6%

profile of v2, /device:TPU:12, one launch (start us, length us, event | category | flops | bytes accessed | tf_op | source)
XLA Modules:
  0.0 152.2 jit_solution(14997633091417009090)
XLA Ops:
  0.0 5.1 %collective-permute-start.18 = (f32[2,384,1024]{2,1,0:T(8,128)}, f32[2,384,1024]{2,1,0:T(8,128)S(1)}, u32[]{:S(2)}, u32[]{:S(2)}) collective-permute-start(f32[2,384,1024]{2,1,0:T(8,128)} %bitcast.5), channel_id=1, source_target_pairs={{0,25},{1,26},{2,95},{3,24},{4,29},{5,30},{6,91},{7,28},{8,48},{9,... | collective-permute-start | bytes 9437192 | tf_op jit(solution)/shard_map/ppermute | solution.py:58
  5.1 1.9 %collective-permute-start.20 = (f32[2,384,1024]{2,1,0:T(8,128)}, f32[2,384,1024]{2,1,0:T(8,128)}, u32[]{:S(2)}, u32[]{:S(2)}) collective-permute-start(f32[2,384,1024]{2,1,0:T(8,128)} %bitcast.6), channel_id=1, source_target_pairs={{0,3},{1,4},{2,1},{3,2},{4,7},{5,0},{6,5},{7,6},{16,19},{17,84},{1... | collective-permute-start | bytes 9437192 | tf_op jit(solution)/shard_map/ppermute | solution.py:58
  7.0 1.3 fusion
  9.6 32.4 %conditional.1 = (f32[1,128]{1,0:T(1,128)}, f32[1,128]{1,0:T(1,128)}) conditional(s32[]{:T(128)} %bitcast.1, f32[1,128]{1,0:T(1,128)} %bitcast.7, f32[1,128]{1,0:T(1,128)} %bitcast.8, f32[1,128]{1,0:T(1,128)} %bitcast.9, f32[1,128]{1,0:T(1,128)} %bitcast.10, f32[1,128]{1,0:T(1,128)} %bitcast.11, ...), branch_computations={%region_0.0_spmd, %region_1.0_spmd, %region_2.0_spmd, %region_3.0_... | conditional | bytes 4192 | solution.py:321
  9.6 2.3 %collective-permute-start.7 = (f32[1,128]{1,0:T(1,128)}, f32[1,128]{1,0:T(1,128)}, u32[]{:S(2)}, u32[]{:S(2)}) collective-permute-start(f32[1,128]{1,0:T(1,128)} %param.3), channel_id=1, source_target_pairs={{0,118},{1,115},{2,52},{3,113},{4,114},{5,119},{6,48},{7,117},{8,1... | collective-permute-start | bytes 1544 | tf_op jit(solution)/shard_map/cond/branch_3_fun/ppermute | solution.py:58
  12.0 30.1 %collective-permute-done.7 = f32[1,128]{1,0:T(1,128)} collective-permute-done((f32[1,128]{1,0:T(1,128)}, f32[1,128]{1,0:T(1,128)}, u32[]{:S(2)}, u32[]{:S(2)}) %collective-permute-start.7) | collective-permute-done | bytes 544 | tf_op jit(solution)/shard_map/cond/branch_3_fun/ppermute | solution.py:58
  42.1 1.5 collective-permute-start.19
  43.5 4.9 %collective-permute-start.22 = (f32[1,8]{1,0:T(1,128)}, f32[1,8]{1,0:T(1,128)S(1)}, u32[]{:S(2)}, u32[]{:S(2)}) collective-permute-start(f32[1,8]{1,0:T(1,128)} %bitcast.16), channel_id=1, source_target_pairs={{0,3},{1,4},{2,1},{3,2},{4,7},{5,0},{6,5},{7,6},{8,56},{9,125},{10... | collective-permute-start | bytes 104 | tf_op jit(solution)/shard_map/ppermute | solution.py:58
  48.5 1.9 %shard_map.47 = (f32[2,384,512]{2,1,0:T(8,128)S(1)}, f32[2,384,512]{2,1,0:T(8,128)S(1)}) custom-call(f32[2,384,1024]{2,1,0:T(8,128)} %collective-permute-done.20.if_lower, f32[2,384,1024]{2,1,0:T(8,128)S(1)} %collective-permute-done.18.if_lower.if_upper), custom_call_target="tpu_custom_call" | custom-call | bytes 6291456 | tf_op jit(solution)/shard_map/pallas_call | solution.py:181
  50.4 3.3 %collective-permute-done.21.occ_a = f32[1,8]{1,0:T(1,128)S(1)} collective-permute-done((f32[1,8]{1,0:T(1,128)}, f32[1,8]{1,0:T(1,128)S(1)}, u32[]{:S(2)}, u32[]{:S(2)}) %collective-permute-start.21) | collective-permute-done | bytes 64 | tf_op jit(solution)/shard_map/ppermute | solution.py:58
  53.7 0.8 shard_map.48
  54.5 0.6 shard_map.46
  55.2 6.4 %shard_map.49 = (f32[2,384,512]{2,1,0:T(8,128)S(1)}, f32[2,384,512]{2,1,0:T(8,128)S(1)}) custom-call(f32[2,384,512]{2,1,0:T(8,128)S(1)} %get-tuple-element.48.refs_0_, f32[2,384,512]{2,1,0:T(8,128)S(1)} %get-tuple-element.43.refs_1_, f32[512,1]{1,0:T(8,128)S(1)} %get-tuple-element.49.refs_2_, f32[1,512]{1,0:T(1,128)S(1)} %get-tuple-element.47.refs_3_), custom_call_target="tpu_custom_call" | custom-call | flops 5435817984 | bytes 6291456 | tf_op jit(solution)/shard_map/pallas_call | solution.py:129
  61.6 6.5 %shard_map.50 = (f32[2,384,512]{2,1,0:T(8,128)S(1)}, f32[2,384,512]{2,1,0:T(8,128)S(1)}) custom-call(f32[2,384,512]{2,1,0:T(8,128)S(1)} %get-tuple-element.42.refs_0_, f32[2,384,512]{2,1,0:T(8,128)S(1)} %get-tuple-element.43.refs_1_, f32[512,1]{1,0:T(8,128)S(1)} %get-tuple-element.46.refs_2_, f32[1,512]{1,0:T(1,128)S(1)} %get-tuple-element.47.refs_3_, ...), custom_call_target="tpu_custom_call" | custom-call | flops 5435817984 | bytes 6291456 | tf_op jit(solution)/shard_map/pallas_call | solution.py:129
  68.2 6.8 %shard_map.51 = (f32[2,384,512]{2,1,0:T(8,128)S(1)}, f32[2,384,512]{2,1,0:T(8,128)S(1)}) custom-call(f32[2,384,512]{2,1,0:T(8,128)S(1)} %get-tuple-element.42.refs_0_, f32[2,384,512]{2,1,0:T(8,128)S(1)} %get-tuple-element.52.refs_1_, f32[512,1]{1,0:T(8,128)S(1)} %get-tuple-element.46.refs_2_, f32[1,512]{1,0:T(1,128)S(1)} %get-tuple-element.53.refs_3_, ...), custom_call_target="tpu_custom_call" | custom-call | flops 5435817984 | bytes 6291456 | tf_op jit(solution)/shard_map/pallas_call | solution.py:129
  74.9 0.1 collective-permute-start.25
  75.0 6.5 %shard_map.52 = (f32[2,384,512]{2,1,0:T(8,128)S(1)}, f32[2,384,512]{2,1,0:T(8,128)S(1)}) custom-call(f32[2,384,512]{2,1,0:T(8,128)S(1)} %get-tuple-element.48.refs_0_, f32[2,384,512]{2,1,0:T(8,128)S(1)} %get-tuple-element.52.refs_1_, f32[512,1]{1,0:T(8,128)S(1)} %get-tuple-element.49.refs_2_, f32[1,512]{1,0:T(1,128)S(1)} %get-tuple-element.53.refs_3_, ...), custom_call_target="tpu_custom_call" | custom-call | flops 5435817984 | bytes 6291456 | tf_op jit(solution)/shard_map/pallas_call | solution.py:129
  81.6 0.8 collective-permute-start.28
  82.4 1.3 collective-permute-start.23
  83.6 0.5 shard_map.53
  84.1 1.3 collective-permute-start.30
  85.4 0.7 collective-permute-start.31
  86.2 1.4 collective-permute-start.26
  87.6 1.3 collective-permute-start.29
  88.9 27.3 %collective-permute-done.23.early = f32[2,384,512]{2,1,0:T(8,128)S(1)} collective-permute-done((f32[2,384,512]{2,1,0:T(8,128)S(1)}, f32[2,384,512]{2,1,0:T(8,128)S(1)}, u32[]{:S(2)}, u32[]{:S(2)}) %collective-permute-start.23) | collective-permute-done | bytes 1572896 | tf_op jit(solution)/shard_map/ppermute | solution.py:58
  116.1 1.4 collective-permute-start.27
  117.5 16.6 %collective-permute-done.30.back_re = f32[384,512]{1,0:T(8,128)S(1)} collective-permute-done((f32[384,512]{1,0:T(8,128)S(1)}, f32[384,512]{1,0:T(8,128)S(1)}, u32[]{:S(2)}, u32[]{:S(2)}) %collective-permute-start.30) | collective-permute-done | bytes 786464 | tf_op jit(solution)/shard_map/ppermute | solution.py:58
  134.1 1.3 collective-permute-start.24
  135.4 1.3 collective-permute-start.32
  136.8 2.7 %collective-permute-done.24.lowered = f32[2,384,512]{2,1,0:T(8,128)S(1)} collective-permute-done((f32[2,384,512]{2,1,0:T(8,128)S(1)}, f32[2,384,512]{2,1,0:T(8,128)S(1)}, u32[]{:S(2)}, u32[]{:S(2)}) %collective-permute-start.24) | collective-permute-done | bytes 1572896 | tf_op jit(solution)/shard_map/ppermute | solution.py:58
  139.4 10.8 %collective-permute-done.32.back_im = f32[384,512]{1,0:T(8,128)S(1)} collective-permute-done((f32[384,512]{1,0:T(8,128)S(1)}, f32[384,512]{1,0:T(8,128)S(1)}, u32[]{:S(2)}, u32[]{:S(2)}) %collective-permute-start.32) | collective-permute-done | bytes 786464 | tf_op jit(solution)/shard_map/ppermute | solution.py:58
  150.2 1.8 %shard_map.54 = f32[2,384,1024]{2,1,0:T(8,128)} custom-call(f32[2,384,512]{2,1,0:T(8,128)S(1)} %collective-permute-done.23.early, f32[2,384,512]{2,1,0:T(8,128)S(1)} %collective-permute-done.24.lowered, f32[2,384,512]{2,1,0:T(8,128)S(1)} %collective-permute-done.26.back_a, f32[2,384,512]{2,1,0:T(8,128)S(1)} %collective-permute-done.27.back_b, ...), custom_call_target="tpu_custom_call" | custom-call | tf_op jit(solution)/shard_map/pallas_call | solution.py:270
  (13 shorter events, 0.0 us)
Async XLA Ops:
  0.0 42.1 %collective-permute-start.18 = (f32[2,384,1024]{2,1,0:T(8,128)}, f32[2,384,1024]{2,1,0:T(8,128)S(1)}, u32[]{:S(2)}, u32[]{:S(2)}) collective-permute-start(f32[2,384,1024]{2,1,0:T(8,128)} %bitcast.5), channel_id=1, source_target_pairs={{0,25},{1,26},{2,95},{3,24},{4,29},{5,30},{6,91},{7,28},{8,48},{9,... | collective-permute-start | bytes 9437192 | tf_op jit(solution)/shard_map/ppermute | solution.py:58
  5.1 43.4 %collective-permute-start.20 = (f32[2,384,1024]{2,1,0:T(8,128)}, f32[2,384,1024]{2,1,0:T(8,128)}, u32[]{:S(2)}, u32[]{:S(2)}) collective-permute-start(f32[2,384,1024]{2,1,0:T(8,128)} %bitcast.6), channel_id=1, source_target_pairs={{0,3},{1,4},{2,1},{3,2},{4,7},{5,0},{6,5},{7,6},{16,19},{17,84},{1... | collective-permute-start | bytes 9437192 | tf_op jit(solution)/shard_map/ppermute | solution.py:58
  9.6 32.4 %collective-permute-start.7 = (f32[1,128]{1,0:T(1,128)}, f32[1,128]{1,0:T(1,128)}, u32[]{:S(2)}, u32[]{:S(2)}) collective-permute-start(f32[1,128]{1,0:T(1,128)} %param.3), channel_id=1, source_target_pairs={{0,118},{1,115},{2,52},{3,113},{4,114},{5,119},{6,48},{7,117},{8,1... | collective-permute-start | bytes 1544 | tf_op jit(solution)/shard_map/cond/branch_3_fun/ppermute | solution.py:58
  12.0 30.1 %collective-permute-start.6 = (f32[1,128]{1,0:T(1,128)}, f32[1,128]{1,0:T(1,128)}, u32[]{:S(2)}, u32[]{:S(2)}) collective-permute-start(f32[1,128]{1,0:T(1,128)} %param.3), channel_id=1, source_target_pairs={{0,76},{1,73},{2,74},{3,79},{4,72},{5,77},{6,78},{7,75},{8,103},{9... | collective-permute-start | bytes 1544 | tf_op jit(solution)/shard_map/cond/branch_3_fun/ppermute | solution.py:58
  42.1 12.5 %collective-permute-start.19 = (f32[2,384,1024]{2,1,0:T(8,128)S(1)}, f32[2,384,1024]{2,1,0:T(8,128)S(1)}, u32[]{:S(2)}, u32[]{:S(2)}) collective-permute-start(f32[2,384,1024]{2,1,0:T(8,128)S(1)} %collective-permute-done.18.if_lower.if_upper), channel_id=1, source_target_pairs={{0,8},{1,9},{2,10},{3,11},{4,12},{5,13},{6,14},{7,15},{16,24},{17,... | collective-permute-start | bytes 9437192 | tf_op jit(solution)/shard_map/ppermute | solution.py:58
  43.5 6.9 %collective-permute-start.22 = (f32[1,8]{1,0:T(1,128)}, f32[1,8]{1,0:T(1,128)S(1)}, u32[]{:S(2)}, u32[]{:S(2)}) collective-permute-start(f32[1,8]{1,0:T(1,128)} %bitcast.16), channel_id=1, source_target_pairs={{0,3},{1,4},{2,1},{3,2},{4,7},{5,0},{6,5},{7,6},{8,56},{9,125},{10... | collective-permute-start | bytes 104 | tf_op jit(solution)/shard_map/ppermute | solution.py:58
  48.5 5.2 %collective-permute-start.21 = (f32[1,8]{1,0:T(1,128)}, f32[1,8]{1,0:T(1,128)S(1)}, u32[]{:S(2)}, u32[]{:S(2)}) collective-permute-start(f32[1,8]{1,0:T(1,128)} %bitcast.17), channel_id=1, source_target_pairs={{0,25},{1,26},{2,95},{3,24},{4,29},{5,30},{6,91},{7,28},{8,48},{9,... | collective-permute-start | bytes 104 | tf_op jit(solution)/shard_map/ppermute | solution.py:58
  74.9 8.7 %collective-permute-start.25 = (f32[2,384,512]{2,1,0:T(8,128)S(1)}, f32[2,384,512]{2,1,0:T(8,128)S(1)}, u32[]{:S(2)}, u32[]{:S(2)}) collective-permute-start(f32[2,384,512]{2,1,0:T(8,128)S(1)} %get-tuple-element.58), channel_id=1, source_target_pairs={{0,8},{1,9},{2,10},{3,11},{4,12},{5,13},{6,14},{7,15},{8,0},{9,1},... | collective-permute-start | bytes 4718600 | tf_op jit(solution)/shard_map/ppermute | solution.py:58
  81.6 6.0 %collective-permute-start.28 = (f32[2,384,512]{2,1,0:T(8,128)S(1)}, f32[2,384,512]{2,1,0:T(8,128)S(1)}, u32[]{:S(2)}, u32[]{:S(2)}) collective-permute-start(f32[2,384,512]{2,1,0:T(8,128)S(1)} %get-tuple-element.59.to_s), channel_id=1, source_target_pairs={{0,4},{4,0},{16,84},{20,80},{27,95},{31,91},{32,100},{36,96},{43,1... | collective-permute-start | bytes 4718600 | tf_op jit(solution)/shard_map/ppermute | solution.py:58
  82.4 33.8 %collective-permute-start.23 = (f32[2,384,512]{2,1,0:T(8,128)S(1)}, f32[2,384,512]{2,1,0:T(8,128)S(1)}, u32[]{:S(2)}, u32[]{:S(2)}) collective-permute-start(f32[2,384,512]{2,1,0:T(8,128)S(1)} %get-tuple-element.51), channel_id=1, source_target_pairs={{0,13},{1,10},{2,11},{3,8},{4,9},{5,14},{6,15},{7,12},{8,51},{9,48... | collective-permute-start | bytes 4718600 | tf_op jit(solution)/shard_map/ppermute | solution.py:58
  84.1 50.0 %collective-permute-start.30 = (f32[384,512]{1,0:T(8,128)S(1)}, f32[384,512]{1,0:T(8,128)S(1)}, u32[]{:S(2)}, u32[]{:S(2)}) collective-permute-start(f32[384,512]{1,0:T(8,128)S(1)} %get-tuple-element.62), channel_id=1, source_target_pairs={{11,54},{15,50},{17,82},{21,86},{75,118},{79,114},{81,18},{85,22}} | collective-permute-start | bytes 2359304 | tf_op jit(solution)/shard_map/ppermute | solution.py:58
  85.4 50.0 %collective-permute-start.31 = (f32[384,512]{1,0:T(8,128)S(1)}, f32[384,512]{1,0:T(8,128)S(1)}, u32[]{:S(2)}, u32[]{:S(2)}) collective-permute-start(f32[384,512]{1,0:T(8,128)S(1)} %get-tuple-element.63), channel_id=1, source_target_pairs={{11,55},{15,51},{17,88},{21,92},{75,119},{79,115},{81,24},{85,28}} | collective-permute-start | bytes 2359304 | tf_op jit(solution)/shard_map/ppermute | solution.py:58
  86.2 50.6 %collective-permute-start.26 = (f32[2,384,512]{2,1,0:T(8,128)S(1)}, f32[2,384,512]{2,1,0:T(8,128)S(1)}, u32[]{:S(2)}, u32[]{:S(2)}) collective-permute-start(f32[2,384,512]{2,1,0:T(8,128)S(1)} %get-tuple-element.60), channel_id=1, source_target_pairs={{0,24},{1,29},{2,30},{3,27},{4,28},{5,25},{6,26},{7,31},{8,51},{9,... | collective-permute-start | bytes 4718600 | tf_op jit(solution)/shard_map/ppermute | solution.py:62
  87.6 49.2 %collective-permute-start.29 = (f32[2,384,512]{2,1,0:T(8,128)S(1)}, f32[2,384,512]{2,1,0:T(8,128)S(1)}, u32[]{:S(2)}, u32[]{:S(2)}) collective-permute-start(f32[2,384,512]{2,1,0:T(8,128)S(1)} %collective-permute-done.28), channel_id=1, source_target_pairs={{0,1},{4,5},{16,17},{20,21},{27,2},{31,6},{32,33},{36,37},{43,18},... | collective-permute-start | bytes 4718600 | tf_op jit(solution)/shard_map/ppermute | solution.py:58
  116.1 20.6 %collective-permute-start.27 = (f32[2,384,512]{2,1,0:T(8,128)S(1)}, f32[2,384,512]{2,1,0:T(8,128)S(1)}, u32[]{:S(2)}, u32[]{:S(2)}) collective-permute-start(f32[2,384,512]{2,1,0:T(8,128)S(1)} %get-tuple-element.61), channel_id=1, source_target_pairs={{1,2},{2,3},{3,0},{5,6},{6,7},{7,4},{8,24},{9,29},{10,30},{11,27},... | collective-permute-start | bytes 4718600 | tf_op jit(solution)/shard_map/ppermute | solution.py:62
  134.1 5.3 %collective-permute-start.24 = (f32[2,384,512]{2,1,0:T(8,128)S(1)}, f32[2,384,512]{2,1,0:T(8,128)S(1)}, u32[]{:S(2)}, u32[]{:S(2)}) collective-permute-start(f32[2,384,512]{2,1,0:T(8,128)S(1)} %collective-permute-done.23.early), channel_id=1, source_target_pairs={{8,0},{9,1},{10,2},{11,3},{12,4},{13,5},{14,6},{15,7},{24,16},{25,... | collective-permute-start | bytes 4718600 | tf_op jit(solution)/shard_map/ppermute | solution.py:58
  135.4 14.8 %collective-permute-start.32 = (f32[384,512]{1,0:T(8,128)S(1)}, f32[384,512]{1,0:T(8,128)S(1)}, u32[]{:S(2)}, u32[]{:S(2)}) collective-permute-start(f32[384,512]{1,0:T(8,128)S(1)} %collective-permute-done.31), channel_id=1, source_target_pairs={{24,18},{28,22},{51,50},{55,54},{88,82},{92,86},{115,114},{119,118}} | collective-permute-start | bytes 2359304 | tf_op jit(solution)/shard_map/ppermute | solution.py:58

commit v3 on v2

--- a/solution.py
+++ b/solution.py
@@ -87,11 +87,11 @@
     return lax.axis_index("kxy") % 2 == 1
 
 
-def block_kernel(has_o, has_w, *refs):
+def block_kernel(has_o, has_w, parted, *refs):
     o_ref, w_ref, gap_o, gap_w, *refs = refs
     old_o = refs.pop(0) if has_o else None
     old_w = refs.pop(0) if has_w else None
-    to_o, to_w, tall, flat = refs
+    to_o, *to_w, tall, flat = refs
     inner = to_o.shape[1]
 
     a, b = o_ref[0], o_ref[1]
@@ -118,19 +118,28 @@
     bq = product(flat[1], right(q, 0), 1, 0)
     both = product(flat[2], right(p - q, 0), 1, 0)
     re, im = ap + bq, both - ap + bq
-    to_w[0] = re + old_w[0] if has_w else re
-    to_w[1] = im + old_w[1] if has_w else im
-
-
-def block(o, w, gap_o, gap_w, old_o=None, old_w=None):
+    re = re + old_w[0] if has_w else re
+    im = im + old_w[1] if has_w else im
+    if parted:
+        to_w[0][...] = re
+        to_w[1][...] = im
+    else:
+        to_w[0][0] = re
+        to_w[0][1] = im
+
+
+def block(o, w, gap_o, gap_w, old_o=None, old_w=None, parted=False):
     parts, inner, half = o.shape
     old = [x for x in (old_o, old_w) if x is not None]
+    whole = jax.ShapeDtypeStruct((parts, inner, half), jnp.float32)
+    part = jax.ShapeDtypeStruct((inner, half), jnp.float32)
+    out_shape = (whole, part, part) if parted else (whole, whole)
     spec = pl.BlockSpec(memory_space=pltpu.VMEM)
     return pl.pallas_call(
-        functools.partial(block_kernel, old_o is not None, old_w is not None),
-        out_shape=(jax.ShapeDtypeStruct((parts, inner, half), jnp.float32),) * 2,
+        functools.partial(block_kernel, old_o is not None, old_w is not None, parted),
+        out_shape=out_shape,
         in_specs=[spec] * (4 + len(old)),
-        out_specs=(spec, spec),
+        out_specs=(spec,) * len(out_shape),
         scratch_shapes=[
             pltpu.VMEM((3, half, 3 * inner), jnp.bfloat16),
             pltpu.VMEM((3, inner, 3 * half), jnp.bfloat16),
@@ -222,30 +231,26 @@
     return out[:2], out[2:]
 
 
-def merge_kernel(to_a, met, to_s, for_a, for_b, for_re, for_im):
-    own = to_a[...] + met[...]
-    other = to_s[...]
+def merge_kernel(to_a, met, re, im, for_a, for_b):
     upper = on_upper()
-    for_a[...] = jnp.where(upper, other, own)
-    for_b[...] = jnp.where(upper, own, other)
-    for_re[...] = other[0]
-    for_im[...] = other[1]
-
-
-def merge(to_a, met, to_s):
+    for i, other in enumerate((re[...], im[...])):
+        own = to_a[i] + met[i]
+        for_a[i] = jnp.where(upper, other, own)
+        for_b[i] = jnp.where(upper, own, other)
+
+
+def merge(to_a, met, re, im):
     spec = pl.BlockSpec(memory_space=pltpu.VMEM)
-    whole = jax.ShapeDtypeStruct(to_a.shape, to_a.dtype)
-    part = jax.ShapeDtypeStruct(to_a.shape[1:], to_a.dtype)
     return pl.pallas_call(
         merge_kernel,
-        out_shape=(whole, whole, part, part),
-        in_specs=[spec] * 3,
-        out_specs=(spec,) * 4,
-        compiler_params=pltpu.CompilerParams(vmem_limit_bytes=LIMIT),
-    )(to_a, met, to_s)
-
-
-def finish_kernel(early, lowered, back_a, back_b, hop, back_re, back_im, out, held, sems):
+        out_shape=(jax.ShapeDtypeStruct(to_a.shape, to_a.dtype),) * 2,
+        in_specs=[spec] * 4,
+        out_specs=(spec, spec),
+        compiler_params=pltpu.CompilerParams(vmem_limit_bytes=LIMIT),
+    )(to_a, met, re, im)
+
+
+def finish_kernel(early, lowered, back_a, back_b, hop_re, hop_im, back_re, back_im, out, held, sems):
     half = back_a.shape[2]
     steps = sems.shape[0]
     rows = back_a.shape[1] // steps
@@ -255,9 +260,9 @@
         at = pl.ds(i * rows, rows)
         a, b = back_a[:, at], back_b[:, at]
         held[:, at, :half] = -jnp.where(upper, a, early[:, at] + lowered[:, at])
-        even = a + b + hop[:, at]
-        held[0, at, half:] = -jnp.where(upper, b[0], even[0] + back_re[at])
-        held[1, at, half:] = -jnp.where(upper, b[1], even[1] + back_im[at])
+        even = a + b
+        held[0, at, half:] = -jnp.where(upper, b[0], even[0] + hop_re[at] + back_re[at])
+        held[1, at, half:] = -jnp.where(upper, b[1], even[1] + hop_im[at] + back_im[at])
         copies.append(pltpu.make_async_copy(held.at[:, at], out.at[:, at], sems.at[i]))
         copies[-1].start()
     for copy in copies:
@@ -270,7 +275,7 @@
     return pl.pallas_call(
         finish_kernel,
         out_shape=jax.ShapeDtypeStruct(shape, backs[0].dtype),
-        in_specs=[pl.BlockSpec(memory_space=pltpu.VMEM)] * 7,
+        in_specs=[pl.BlockSpec(memory_space=pltpu.VMEM)] * 8,
         out_specs=pl.BlockSpec(memory_space=pl.ANY),
         scratch_shapes=[pltpu.VMEM(shape, backs[0].dtype), pltpu.SemaphoreType.DMA((6,))],
         compiler_params=pltpu.CompilerParams(vmem_limit_bytes=LIMIT),
@@ -330,17 +335,18 @@
     back_early = move(to_f, route_early)
     to_b, to_s = block(o[1], w[1], gap_o[1], gap_w[1], old_o=to_b)
     met = move(to_b, cores)
-    to_a, to_s = block(o[0], w[1], gap_o[0], gap_w[1], to_a, to_s)
-    middle = move(to_s, first_hop)
-    for_a, for_b, for_re, for_im = merge(to_a, met, to_s)
-    part = move(for_im, part_hop)
+    to_a, re, im = block(o[0], w[1], gap_o[0], gap_w[1], to_a, to_s, parted=True)
+    middle_re = move(re, first_hop)
+    middle_im = move(im, first_hop | part_hop)
+    for_a, for_b = merge(to_a, met, re, im)
     back_a = move_back(for_a, late_a)
     back_b = move_back(for_b, late_b)
-    back_re = move(for_re, straight)
+    back_re = move(re, straight)
+    hop_re = move(middle_re, second_hop)
+    hop_im = move(middle_im, second_hop)
+    back_im = move(middle_im, leave_hop)
     lowered = move(back_early, downward)
-    hop = move(middle, second_hop)
-    back_im = move(part, leave_hop)
-    return finish(back_early, lowered, back_a, back_b, hop, back_re, back_im)[None, None]
+    return finish(back_early, lowered, back_a, back_b, hop_re, hop_im, back_re, back_im)[None, None]
 
 
 def solution(mesh):

time: 153 us -> 154 us (level)
    ppermute x15 -> x16, waiting for transfers between devices: 90.8 us -> 91.6 us  [move(): return lax.ppermute(x, AXES, sorted(route.items()))]
    ppermute x15 -> x16, starting transfers between devices: 23.8 us -> 23.8 us  [move(): return lax.ppermute(x, AXES, sorted(route.items()))]
  transfers between devices with their start and end apart: 17 -> 18, of which waited for: 6 -> 5; matrix products, arithmetic and copies ran while one was open for 1% -> 1% of each run, Pallas kernels for 6% -> 6%
where the time goes in v3:
time: 154 us
  waiting for transfers between devices  91.6 us (59%)
  Pallas kernels  31.8 us (21%)
  starting transfers between devices  27.1 us (18%)
  between operations  1.69 us (1%)
    ppermute x16, waiting for transfers between devices, move(): return lax.ppermute(x, AXES, sorted(route.items()))  91.6 us
    pallas_call x4, Pallas kernels, block(): pl.pallas_call(functools.partial(block_kernel, old_o is not None, old_w i...  26.3 us
    ppermute x16, starting transfers between devices, move(): return lax.ppermute(x, AXES, sorted(route.items()))  23.8 us
    ppermute x2, starting transfers between devices, move_back(): return lax.ppermute(x, AXES, sorted(((t, s) for s, t in route.items())))  3.22 us
  transfers between devices with their start and end apart: 18, of which 5 were waited for; matrix products, arithmetic and copies ran while one was open for 1% of the time, Pallas kernels for 6%

profile of v3, /device:TPU:12, one launch (start us, length us, event | category | flops | bytes accessed | tf_op | source)
XLA Modules:
  0.0 153.6 jit_solution(9036689612104218880)
XLA Ops:
  0.0 5.1 %collective-permute-start.18 = (f32[2,384,1024]{2,1,0:T(8,128)}, f32[2,384,1024]{2,1,0:T(8,128)S(1)}, u32[]{:S(2)}, u32[]{:S(2)}) collective-permute-start(f32[2,384,1024]{2,1,0:T(8,128)} %bitcast.5), channel_id=1, source_target_pairs={{0,25},{1,26},{2,95},{3,24},{4,29},{5,30},{6,91},{7,28},{8,48},{9,... | collective-permute-start | bytes 9437192 | tf_op jit(solution)/shard_map/ppermute | solution.py:58
  5.1 1.9 %collective-permute-start.20 = (f32[2,384,1024]{2,1,0:T(8,128)}, f32[2,384,1024]{2,1,0:T(8,128)}, u32[]{:S(2)}, u32[]{:S(2)}) collective-permute-start(f32[2,384,1024]{2,1,0:T(8,128)} %bitcast.6), channel_id=1, source_target_pairs={{0,3},{1,4},{2,1},{3,2},{4,7},{5,0},{6,5},{7,6},{16,19},{17,84},{1... | collective-permute-start | bytes 9437192 | tf_op jit(solution)/shard_map/ppermute | solution.py:58
  7.0 1.3 fusion
  9.7 32.4 %conditional.1 = (f32[1,128]{1,0:T(1,128)}, f32[1,128]{1,0:T(1,128)}) conditional(s32[]{:T(128)} %bitcast.1, f32[1,128]{1,0:T(1,128)} %bitcast.7, f32[1,128]{1,0:T(1,128)} %bitcast.8, f32[1,128]{1,0:T(1,128)} %bitcast.9, f32[1,128]{1,0:T(1,128)} %bitcast.10, f32[1,128]{1,0:T(1,128)} %bitcast.11, ...), branch_computations={%region_0.0_spmd, %region_1.0_spmd, %region_2.0_spmd, %region_3.0_... | conditional | bytes 4192 | solution.py:326
  9.7 2.3 %collective-permute-start.7 = (f32[1,128]{1,0:T(1,128)}, f32[1,128]{1,0:T(1,128)}, u32[]{:S(2)}, u32[]{:S(2)}) collective-permute-start(f32[1,128]{1,0:T(1,128)} %param.3), channel_id=1, source_target_pairs={{0,118},{1,115},{2,52},{3,113},{4,114},{5,119},{6,48},{7,117},{8,1... | collective-permute-start | bytes 1544 | tf_op jit(solution)/shard_map/cond/branch_3_fun/ppermute | solution.py:58
  12.0 30.0 %collective-permute-done.7 = f32[1,128]{1,0:T(1,128)} collective-permute-done((f32[1,128]{1,0:T(1,128)}, f32[1,128]{1,0:T(1,128)}, u32[]{:S(2)}, u32[]{:S(2)}) %collective-permute-start.7) | collective-permute-done | bytes 544 | tf_op jit(solution)/shard_map/cond/branch_3_fun/ppermute | solution.py:58
  42.1 1.5 collective-permute-start.19
  43.5 4.9 %collective-permute-start.22 = (f32[1,8]{1,0:T(1,128)}, f32[1,8]{1,0:T(1,128)S(1)}, u32[]{:S(2)}, u32[]{:S(2)}) collective-permute-start(f32[1,8]{1,0:T(1,128)} %bitcast.16), channel_id=1, source_target_pairs={{0,3},{1,4},{2,1},{3,2},{4,7},{5,0},{6,5},{7,6},{8,56},{9,125},{10... | collective-permute-start | bytes 104 | tf_op jit(solution)/shard_map/ppermute | solution.py:58
  48.5 1.9 %shard_map.47 = (f32[2,384,512]{2,1,0:T(8,128)S(1)}, f32[2,384,512]{2,1,0:T(8,128)S(1)}) custom-call(f32[2,384,1024]{2,1,0:T(8,128)} %collective-permute-done.20.if_lower, f32[2,384,1024]{2,1,0:T(8,128)S(1)} %collective-permute-done.18.if_lower.if_upper), custom_call_target="tpu_custom_call" | custom-call | bytes 6291456 | tf_op jit(solution)/shard_map/pallas_call | solution.py:190
  50.4 3.3 %collective-permute-done.21.occ_a = f32[1,8]{1,0:T(1,128)S(1)} collective-permute-done((f32[1,8]{1,0:T(1,128)}, f32[1,8]{1,0:T(1,128)S(1)}, u32[]{:S(2)}, u32[]{:S(2)}) %collective-permute-start.21) | collective-permute-done | bytes 64 | tf_op jit(solution)/shard_map/ppermute | solution.py:58
  53.7 0.8 shard_map.48
  54.5 0.6 shard_map.46
  55.2 6.4 %shard_map.49 = (f32[2,384,512]{2,1,0:T(8,128)S(1)}, f32[2,384,512]{2,1,0:T(8,128)S(1)}) custom-call(f32[2,384,512]{2,1,0:T(8,128)S(1)} %get-tuple-element.47.refs_0_, f32[2,384,512]{2,1,0:T(8,128)S(1)} %get-tuple-element.42.refs_1_, f32[512,1]{1,0:T(8,128)S(1)} %get-tuple-element.48.refs_2_, f32[1,512]{1,0:T(1,128)S(1)} %get-tuple-element.46.refs_3_), custom_call_target="tpu_custom_call" | custom-call | flops 5435817984 | bytes 6291456 | tf_op jit(solution)/shard_map/pallas_call | solution.py:138
  61.6 6.5 %shard_map.50 = (f32[2,384,512]{2,1,0:T(8,128)S(1)}, f32[2,384,512]{2,1,0:T(8,128)S(1)}) custom-call(f32[2,384,512]{2,1,0:T(8,128)S(1)} %get-tuple-element.41.refs_0_, f32[2,384,512]{2,1,0:T(8,128)S(1)} %get-tuple-element.42.refs_1_, f32[512,1]{1,0:T(8,128)S(1)} %get-tuple-element.45.refs_2_, f32[1,512]{1,0:T(1,128)S(1)} %get-tuple-element.46.refs_3_, ...), custom_call_target="tpu_custom_call" | custom-call | flops 5435817984 | bytes 6291456 | tf_op jit(solution)/shard_map/pallas_call | solution.py:138
  68.1 6.8 %shard_map.51 = (f32[2,384,512]{2,1,0:T(8,128)S(1)}, f32[2,384,512]{2,1,0:T(8,128)S(1)}) custom-call(f32[2,384,512]{2,1,0:T(8,128)S(1)} %get-tuple-element.41.refs_0_, f32[2,384,512]{2,1,0:T(8,128)S(1)} %get-tuple-element.51.refs_1_, f32[512,1]{1,0:T(8,128)S(1)} %get-tuple-element.45.refs_2_, f32[1,512]{1,0:T(1,128)S(1)} %get-tuple-element.52.refs_3_, ...), custom_call_target="tpu_custom_call" | custom-call | flops 5435817984 | bytes 6291456 | tf_op jit(solution)/shard_map/pallas_call | solution.py:138
  74.9 0.1 collective-permute-start.25
  75.0 0.1 collective-permute-start.23
  75.1 6.6 %shard_map.52 = (f32[2,384,512]{2,1,0:T(8,128)S(1)}, f32[384,512]{1,0:T(8,128)S(1)}, f32[384,512]{1,0:T(8,128)S(1)}) custom-call(f32[2,384,512]{2,1,0:T(8,128)S(1)} %get-tuple-element.47.refs_0_, f32[2,384,512]{2,1,0:T(8,128)S(1)} %get-tuple-element.51.refs_1_, f32[512,1]{1,0:T(8,128)S(1)} %get-tuple-element.48.refs_2_, ...), custom_call_target="tpu_custom_call" | custom-call | flops 5435817984 | bytes 6291456 | tf_op jit(solution)/shard_map/pallas_call | solution.py:138
  81.7 0.7 collective-permute-start.30
  82.5 1.3 collective-permute-start.32
  83.8 0.7 collective-permute-start.28
  84.5 1.3 collective-permute-start.33
  85.8 0.3 shard_map.53
  86.1 1.8 %collective-permute-start.26 = (f32[2,384,512]{2,1,0:T(8,128)S(1)}, f32[2,384,512]{2,1,0:T(8,128)S(1)}, u32[]{:S(2)}, u32[]{:S(2)}) collective-permute-start(f32[2,384,512]{2,1,0:T(8,128)S(1)} %get-tuple-element.60), channel_id=1, source_target_pairs={{0,24},{1,29},{2,30},{3,27},{4,28},{5,25},{6,26},{7,31},{8,51},{9,... | collective-permute-start | bytes 4718600 | tf_op jit(solution)/shard_map/ppermute | solution.py:62
  88.0 38.2 %collective-permute-done.32.back_re = f32[384,512]{1,0:T(8,128)S(1)} collective-permute-done((f32[384,512]{1,0:T(8,128)S(1)}, f32[384,512]{1,0:T(8,128)S(1)}, u32[]{:S(2)}, u32[]{:S(2)}) %collective-permute-start.32) | collective-permute-done | bytes 786464 | tf_op jit(solution)/shard_map/ppermute | solution.py:58
  126.2 1.4 collective-permute-start.27
  127.6 1.3 collective-permute-start.24
  128.9 1.3 collective-permute-start.31
  130.2 1.3 collective-permute-start.29
  131.5 11.6 %collective-permute-done.31.hop_im = f32[384,512]{1,0:T(8,128)S(1)} collective-permute-done((f32[384,512]{1,0:T(8,128)S(1)}, f32[384,512]{1,0:T(8,128)S(1)}, u32[]{:S(2)}, u32[]{:S(2)}) %collective-permute-start.31) | collective-permute-done | bytes 786464 | tf_op jit(solution)/shard_map/ppermute | solution.py:58
  143.1 8.4 %collective-permute-done.29.hop_re = f32[384,512]{1,0:T(8,128)S(1)} collective-permute-done((f32[384,512]{1,0:T(8,128)S(1)}, f32[384,512]{1,0:T(8,128)S(1)}, u32[]{:S(2)}, u32[]{:S(2)}) %collective-permute-start.29) | collective-permute-done | bytes 786464 | tf_op jit(solution)/shard_map/ppermute | solution.py:58
  151.6 1.8 %shard_map.54 = f32[2,384,1024]{2,1,0:T(8,128)} custom-call(f32[2,384,512]{2,1,0:T(8,128)S(1)} %collective-permute-done.23.early, f32[2,384,512]{2,1,0:T(8,128)S(1)} %collective-permute-done.24.lowered, f32[2,384,512]{2,1,0:T(8,128)S(1)} %collective-permute-done.26.back_a, f32[2,384,512]{2,1,0:T(8,128)S(1)} %collective-permute-done.27.back_b, ...), custom_call_target="tpu_custom_call" | custom-call | tf_op jit(solution)/shard_map/pallas_call | solution.py:275
  (15 shorter events, 0.0 us)
Async XLA Ops:
  0.0 42.1 %collective-permute-start.18 = (f32[2,384,1024]{2,1,0:T(8,128)}, f32[2,384,1024]{2,1,0:T(8,128)S(1)}, u32[]{:S(2)}, u32[]{:S(2)}) collective-permute-start(f32[2,384,1024]{2,1,0:T(8,128)} %bitcast.5), channel_id=1, source_target_pairs={{0,25},{1,26},{2,95},{3,24},{4,29},{5,30},{6,91},{7,28},{8,48},{9,... | collective-permute-start | bytes 9437192 | tf_op jit(solution)/shard_map/ppermute | solution.py:58
  5.1 43.4 %collective-permute-start.20 = (f32[2,384,1024]{2,1,0:T(8,128)}, f32[2,384,1024]{2,1,0:T(8,128)}, u32[]{:S(2)}, u32[]{:S(2)}) collective-permute-start(f32[2,384,1024]{2,1,0:T(8,128)} %bitcast.6), channel_id=1, source_target_pairs={{0,3},{1,4},{2,1},{3,2},{4,7},{5,0},{6,5},{7,6},{16,19},{17,84},{1... | collective-permute-start | bytes 9437192 | tf_op jit(solution)/shard_map/ppermute | solution.py:58
  9.7 32.4 %collective-permute-start.7 = (f32[1,128]{1,0:T(1,128)}, f32[1,128]{1,0:T(1,128)}, u32[]{:S(2)}, u32[]{:S(2)}) collective-permute-start(f32[1,128]{1,0:T(1,128)} %param.3), channel_id=1, source_target_pairs={{0,118},{1,115},{2,52},{3,113},{4,114},{5,119},{6,48},{7,117},{8,1... | collective-permute-start | bytes 1544 | tf_op jit(solution)/shard_map/cond/branch_3_fun/ppermute | solution.py:58
  12.0 30.0 %collective-permute-start.6 = (f32[1,128]{1,0:T(1,128)}, f32[1,128]{1,0:T(1,128)}, u32[]{:S(2)}, u32[]{:S(2)}) collective-permute-start(f32[1,128]{1,0:T(1,128)} %param.3), channel_id=1, source_target_pairs={{0,76},{1,73},{2,74},{3,79},{4,72},{5,77},{6,78},{7,75},{8,103},{9... | collective-permute-start | bytes 1544 | tf_op jit(solution)/shard_map/cond/branch_3_fun/ppermute | solution.py:58
  42.1 12.5 %collective-permute-start.19 = (f32[2,384,1024]{2,1,0:T(8,128)S(1)}, f32[2,384,1024]{2,1,0:T(8,128)S(1)}, u32[]{:S(2)}, u32[]{:S(2)}) collective-permute-start(f32[2,384,1024]{2,1,0:T(8,128)S(1)} %collective-permute-done.18.if_lower.if_upper), channel_id=1, source_target_pairs={{0,8},{1,9},{2,10},{3,11},{4,12},{5,13},{6,14},{7,15},{16,24},{17,... | collective-permute-start | bytes 9437192 | tf_op jit(solution)/shard_map/ppermute | solution.py:58
  43.5 6.9 %collective-permute-start.22 = (f32[1,8]{1,0:T(1,128)}, f32[1,8]{1,0:T(1,128)S(1)}, u32[]{:S(2)}, u32[]{:S(2)}) collective-permute-start(f32[1,8]{1,0:T(1,128)} %bitcast.16), channel_id=1, source_target_pairs={{0,3},{1,4},{2,1},{3,2},{4,7},{5,0},{6,5},{7,6},{8,56},{9,125},{10... | collective-permute-start | bytes 104 | tf_op jit(solution)/shard_map/ppermute | solution.py:58
  48.5 5.2 %collective-permute-start.21 = (f32[1,8]{1,0:T(1,128)}, f32[1,8]{1,0:T(1,128)S(1)}, u32[]{:S(2)}, u32[]{:S(2)}) collective-permute-start(f32[1,8]{1,0:T(1,128)} %bitcast.17), channel_id=1, source_target_pairs={{0,25},{1,26},{2,95},{3,24},{4,29},{5,30},{6,91},{7,28},{8,48},{9,... | collective-permute-start | bytes 104 | tf_op jit(solution)/shard_map/ppermute | solution.py:58
  74.9 10.9 %collective-permute-start.25 = (f32[2,384,512]{2,1,0:T(8,128)S(1)}, f32[2,384,512]{2,1,0:T(8,128)S(1)}, u32[]{:S(2)}, u32[]{:S(2)}) collective-permute-start(f32[2,384,512]{2,1,0:T(8,128)S(1)} %get-tuple-element.57), channel_id=1, source_target_pairs={{0,8},{1,9},{2,10},{3,11},{4,12},{5,13},{6,14},{7,15},{8,0},{9,1},... | collective-permute-start | bytes 4718600 | tf_op jit(solution)/shard_map/ppermute | solution.py:58
  75.0 52.6 %collective-permute-start.23 = (f32[2,384,512]{2,1,0:T(8,128)S(1)}, f32[2,384,512]{2,1,0:T(8,128)S(1)}, u32[]{:S(2)}, u32[]{:S(2)}) collective-permute-start(f32[2,384,512]{2,1,0:T(8,128)S(1)} %get-tuple-element.50), channel_id=1, source_target_pairs={{0,13},{1,10},{2,11},{3,8},{4,9},{5,14},{6,15},{7,12},{8,51},{9,48... | collective-permute-start | bytes 4718600 | tf_op jit(solution)/shard_map/ppermute | solution.py:58
  81.7 2.7 %collective-permute-start.30 = (f32[384,512]{1,0:T(8,128)S(1)}, f32[384,512]{1,0:T(8,128)S(1)}, u32[]{:S(2)}, u32[]{:S(2)}) collective-permute-start(f32[384,512]{1,0:T(8,128)S(1)} %get-tuple-element.59.im), channel_id=1, source_target_pairs={{0,4},{4,0},{11,55},{15,51},{16,84},{17,88},{20,80},{21,92},{27,95... | collective-permute-start | bytes 2359304 | tf_op jit(solution)/shard_map/ppermute | solution.py:58
  82.5 43.8 %collective-permute-start.32 = (f32[384,512]{1,0:T(8,128)S(1)}, f32[384,512]{1,0:T(8,128)S(1)}, u32[]{:S(2)}, u32[]{:S(2)}) collective-permute-start(f32[384,512]{1,0:T(8,128)S(1)} %get-tuple-element.58.re), channel_id=1, source_target_pairs={{11,54},{15,50},{17,82},{21,86},{75,118},{79,114},{81,18},{85,22}} | collective-permute-start | bytes 2359304 | tf_op jit(solution)/shard_map/ppermute | solution.py:58
  83.8 45.2 %collective-permute-start.28 = (f32[384,512]{1,0:T(8,128)S(1)}, f32[384,512]{1,0:T(8,128)S(1)}, u32[]{:S(2)}, u32[]{:S(2)}) collective-permute-start(f32[384,512]{1,0:T(8,128)S(1)} %get-tuple-element.58.re), channel_id=1, source_target_pairs={{0,4},{4,0},{16,84},{20,80},{27,95},{31,91},{32,100},{36,96},{43,1... | collective-permute-start | bytes 2359304 | tf_op jit(solution)/shard_map/ppermute | solution.py:58
  84.5 45.7 %collective-permute-start.33 = (f32[384,512]{1,0:T(8,128)S(1)}, f32[384,512]{1,0:T(8,128)S(1)}, u32[]{:S(2)}, u32[]{:S(2)}) collective-permute-start(f32[384,512]{1,0:T(8,128)S(1)} %collective-permute-done.30), channel_id=1, source_target_pairs={{24,18},{28,22},{51,50},{55,54},{88,82},{92,86},{115,114},{119,118}} | collective-permute-start | bytes 2359304 | tf_op jit(solution)/shard_map/ppermute | solution.py:58
  86.1 65.4 %collective-permute-start.26 = (f32[2,384,512]{2,1,0:T(8,128)S(1)}, f32[2,384,512]{2,1,0:T(8,128)S(1)}, u32[]{:S(2)}, u32[]{:S(2)}) collective-permute-start(f32[2,384,512]{2,1,0:T(8,128)S(1)} %get-tuple-element.60), channel_id=1, source_target_pairs={{0,24},{1,29},{2,30},{3,27},{4,28},{5,25},{6,26},{7,31},{8,51},{9,... | collective-permute-start | bytes 4718600 | tf_op jit(solution)/shard_map/ppermute | solution.py:62
  126.2 25.3 %collective-permute-start.27 = (f32[2,384,512]{2,1,0:T(8,128)S(1)}, f32[2,384,512]{2,1,0:T(8,128)S(1)}, u32[]{:S(2)}, u32[]{:S(2)}) collective-permute-start(f32[2,384,512]{2,1,0:T(8,128)S(1)} %get-tuple-element.61), channel_id=1, source_target_pairs={{1,2},{2,3},{3,0},{5,6},{6,7},{7,4},{8,24},{9,29},{10,30},{11,27},... | collective-permute-start | bytes 4718600 | tf_op jit(solution)/shard_map/ppermute | solution.py:62
  127.6 24.0 %collective-permute-start.24 = (f32[2,384,512]{2,1,0:T(8,128)S(1)}, f32[2,384,512]{2,1,0:T(8,128)S(1)}, u32[]{:S(2)}, u32[]{:S(2)}) collective-permute-start(f32[2,384,512]{2,1,0:T(8,128)S(1)} %collective-permute-done.23.early), channel_id=1, source_target_pairs={{8,0},{9,1},{10,2},{11,3},{12,4},{13,5},{14,6},{15,7},{24,16},{25,... | collective-permute-start | bytes 4718600 | tf_op jit(solution)/shard_map/ppermute | solution.py:58
  128.9 14.2 %collective-permute-start.31 = (f32[384,512]{1,0:T(8,128)S(1)}, f32[384,512]{1,0:T(8,128)S(1)}, u32[]{:S(2)}, u32[]{:S(2)}) collective-permute-start(f32[384,512]{1,0:T(8,128)S(1)} %collective-permute-done.30), channel_id=1, source_target_pairs={{0,1},{4,5},{16,17},{20,21},{27,2},{31,6},{32,33},{36,37},{43,18},... | collective-permute-start | bytes 2359304 | tf_op jit(solution)/shard_map/ppermute | solution.py:58
  130.2 21.3 %collective-permute-start.29 = (f32[384,512]{1,0:T(8,128)S(1)}, f32[384,512]{1,0:T(8,128)S(1)}, u32[]{:S(2)}, u32[]{:S(2)}) collective-permute-start(f32[384,512]{1,0:T(8,128)S(1)} %collective-permute-done.28), channel_id=1, source_target_pairs={{0,1},{4,5},{16,17},{20,21},{27,2},{31,6},{32,33},{36,37},{43,18},... | collective-permute-start | bytes 2359304 | tf_op jit(solution)/shard_map/ppermute | solution.py:58

commit v4 on v3

--- a/solution.py
+++ b/solution.py
@@ -336,15 +336,15 @@
     to_b, to_s = block(o[1], w[1], gap_o[1], gap_w[1], old_o=to_b)
     met = move(to_b, cores)
     to_a, re, im = block(o[0], w[1], gap_o[0], gap_w[1], to_a, to_s, parted=True)
-    middle_re = move(re, first_hop)
-    middle_im = move(im, first_hop | part_hop)
+    middle_re = move(re, first_hop | part_hop)
+    middle_im = move(im, first_hop)
     for_a, for_b = merge(to_a, met, re, im)
     back_a = move_back(for_a, late_a)
     back_b = move_back(for_b, late_b)
-    back_re = move(re, straight)
+    back_im = move(im, straight)
     hop_re = move(middle_re, second_hop)
+    back_re = move(middle_re, leave_hop)
     hop_im = move(middle_im, second_hop)
-    back_im = move(middle_im, leave_hop)
     lowered = move(back_early, downward)
     return finish(back_early, lowered, back_a, back_b, hop_re, hop_im, back_re, back_im)[None, None]
 

time: 154 us -> 154 us (level)
  no operation moved by 1% of the time
where the time goes in v4:
time: 154 us
  waiting for transfers between devices  91.6 us (59%)
  Pallas kernels  31.8 us (21%)
  starting transfers between devices  27.1 us (18%)
  between operations  1.69 us (1%)
    ppermute x16, waiting for transfers between devices, move(): return lax.ppermute(x, AXES, sorted(route.items()))  91.6 us
    pallas_call x4, Pallas kernels, block(): pl.pallas_call(functools.partial(block_kernel, old_o is not None, old_w i...  26.3 us
    ppermute x16, starting transfers between devices, move(): return lax.ppermute(x, AXES, sorted(route.items()))  23.8 us
    ppermute x2, starting transfers between devices, move_back(): return lax.ppermute(x, AXES, sorted(((t, s) for s, t in route.items())))  3.22 us
  transfers between devices with their start and end apart: 18, of which 5 were waited for; matrix products, arithmetic and copies ran while one was open for 1% of the time, Pallas kernels for 6%

profile of v4, /device:TPU:12, one launch (start us, length us, event | category | flops | bytes accessed | tf_op | source)
XLA Modules:
  0.0 153.6 jit_solution(10606964314713247056)
XLA Ops:
  0.0 5.1 %collective-permute-start.18 = (f32[2,384,1024]{2,1,0:T(8,128)}, f32[2,384,1024]{2,1,0:T(8,128)S(1)}, u32[]{:S(2)}, u32[]{:S(2)}) collective-permute-start(f32[2,384,1024]{2,1,0:T(8,128)} %bitcast.5), channel_id=1, source_target_pairs={{0,25},{1,26},{2,95},{3,24},{4,29},{5,30},{6,91},{7,28},{8,48},{9,... | collective-permute-start | bytes 9437192 | tf_op jit(solution)/shard_map/ppermute | solution.py:58
  5.1 1.9 %collective-permute-start.20 = (f32[2,384,1024]{2,1,0:T(8,128)}, f32[2,384,1024]{2,1,0:T(8,128)}, u32[]{:S(2)}, u32[]{:S(2)}) collective-permute-start(f32[2,384,1024]{2,1,0:T(8,128)} %bitcast.6), channel_id=1, source_target_pairs={{0,3},{1,4},{2,1},{3,2},{4,7},{5,0},{6,5},{7,6},{16,19},{17,84},{1... | collective-permute-start | bytes 9437192 | tf_op jit(solution)/shard_map/ppermute | solution.py:58
  7.0 1.3 fusion
  9.7 32.4 %conditional.1 = (f32[1,128]{1,0:T(1,128)}, f32[1,128]{1,0:T(1,128)}) conditional(s32[]{:T(128)} %bitcast.1, f32[1,128]{1,0:T(1,128)} %bitcast.7, f32[1,128]{1,0:T(1,128)} %bitcast.8, f32[1,128]{1,0:T(1,128)} %bitcast.9, f32[1,128]{1,0:T(1,128)} %bitcast.10, f32[1,128]{1,0:T(1,128)} %bitcast.11, ...), branch_computations={%region_0.0_spmd, %region_1.0_spmd, %region_2.0_spmd, %region_3.0_... | conditional | bytes 4192 | solution.py:326
  9.7 2.3 %collective-permute-start.7 = (f32[1,128]{1,0:T(1,128)}, f32[1,128]{1,0:T(1,128)}, u32[]{:S(2)}, u32[]{:S(2)}) collective-permute-start(f32[1,128]{1,0:T(1,128)} %param.3), channel_id=1, source_target_pairs={{0,118},{1,115},{2,52},{3,113},{4,114},{5,119},{6,48},{7,117},{8,1... | collective-permute-start | bytes 1544 | tf_op jit(solution)/shard_map/cond/branch_3_fun/ppermute | solution.py:58
  12.0 30.0 %collective-permute-done.7 = f32[1,128]{1,0:T(1,128)} collective-permute-done((f32[1,128]{1,0:T(1,128)}, f32[1,128]{1,0:T(1,128)}, u32[]{:S(2)}, u32[]{:S(2)}) %collective-permute-start.7) | collective-permute-done | bytes 544 | tf_op jit(solution)/shard_map/cond/branch_3_fun/ppermute | solution.py:58
  42.1 1.5 collective-permute-start.19
  43.5 4.9 %collective-permute-start.22 = (f32[1,8]{1,0:T(1,128)}, f32[1,8]{1,0:T(1,128)S(1)}, u32[]{:S(2)}, u32[]{:S(2)}) collective-permute-start(f32[1,8]{1,0:T(1,128)} %bitcast.16), channel_id=1, source_target_pairs={{0,3},{1,4},{2,1},{3,2},{4,7},{5,0},{6,5},{7,6},{8,56},{9,125},{10... | collective-permute-start | bytes 104 | tf_op jit(solution)/shard_map/ppermute | solution.py:58
  48.5 1.9 %shard_map.47 = (f32[2,384,512]{2,1,0:T(8,128)S(1)}, f32[2,384,512]{2,1,0:T(8,128)S(1)}) custom-call(f32[2,384,1024]{2,1,0:T(8,128)} %collective-permute-done.20.if_lower, f32[2,384,1024]{2,1,0:T(8,128)S(1)} %collective-permute-done.18.if_lower.if_upper), custom_call_target="tpu_custom_call" | custom-call | bytes 6291456 | tf_op jit(solution)/shard_map/pallas_call | solution.py:190
  50.4 3.3 %collective-permute-done.21.occ_a = f32[1,8]{1,0:T(1,128)S(1)} collective-permute-done((f32[1,8]{1,0:T(1,128)}, f32[1,8]{1,0:T(1,128)S(1)}, u32[]{:S(2)}, u32[]{:S(2)}) %collective-permute-start.21) | collective-permute-done | bytes 64 | tf_op jit(solution)/shard_map/ppermute | solution.py:58
  53.7 0.8 shard_map.48
  54.5 0.6 shard_map.46
  55.2 6.4 %shard_map.49 = (f32[2,384,512]{2,1,0:T(8,128)S(1)}, f32[2,384,512]{2,1,0:T(8,128)S(1)}) custom-call(f32[2,384,512]{2,1,0:T(8,128)S(1)} %get-tuple-element.47.refs_0_, f32[2,384,512]{2,1,0:T(8,128)S(1)} %get-tuple-element.42.refs_1_, f32[512,1]{1,0:T(8,128)S(1)} %get-tuple-element.48.refs_2_, f32[1,512]{1,0:T(1,128)S(1)} %get-tuple-element.46.refs_3_), custom_call_target="tpu_custom_call" | custom-call | flops 5435817984 | bytes 6291456 | tf_op jit(solution)/shard_map/pallas_call | solution.py:138
  61.6 6.5 %shard_map.50 = (f32[2,384,512]{2,1,0:T(8,128)S(1)}, f32[2,384,512]{2,1,0:T(8,128)S(1)}) custom-call(f32[2,384,512]{2,1,0:T(8,128)S(1)} %get-tuple-element.41.refs_0_, f32[2,384,512]{2,1,0:T(8,128)S(1)} %get-tuple-element.42.refs_1_, f32[512,1]{1,0:T(8,128)S(1)} %get-tuple-element.45.refs_2_, f32[1,512]{1,0:T(1,128)S(1)} %get-tuple-element.46.refs_3_, ...), custom_call_target="tpu_custom_call" | custom-call | flops 5435817984 | bytes 6291456 | tf_op jit(solution)/shard_map/pallas_call | solution.py:138
  68.1 6.8 %shard_map.51 = (f32[2,384,512]{2,1,0:T(8,128)S(1)}, f32[2,384,512]{2,1,0:T(8,128)S(1)}) custom-call(f32[2,384,512]{2,1,0:T(8,128)S(1)} %get-tuple-element.41.refs_0_, f32[2,384,512]{2,1,0:T(8,128)S(1)} %get-tuple-element.51.refs_1_, f32[512,1]{1,0:T(8,128)S(1)} %get-tuple-element.45.refs_2_, f32[1,512]{1,0:T(1,128)S(1)} %get-tuple-element.52.refs_3_, ...), custom_call_target="tpu_custom_call" | custom-call | flops 5435817984 | bytes 6291456 | tf_op jit(solution)/shard_map/pallas_call | solution.py:138
  74.9 0.1 collective-permute-start.25
  75.0 0.1 collective-permute-start.23
  75.1 6.6 %shard_map.52 = (f32[2,384,512]{2,1,0:T(8,128)S(1)}, f32[384,512]{1,0:T(8,128)S(1)}, f32[384,512]{1,0:T(8,128)S(1)}) custom-call(f32[2,384,512]{2,1,0:T(8,128)S(1)} %get-tuple-element.47.refs_0_, f32[2,384,512]{2,1,0:T(8,128)S(1)} %get-tuple-element.51.refs_1_, f32[512,1]{1,0:T(8,128)S(1)} %get-tuple-element.48.refs_2_, ...), custom_call_target="tpu_custom_call" | custom-call | flops 5435817984 | bytes 6291456 | tf_op jit(solution)/shard_map/pallas_call | solution.py:138
  81.7 0.7 collective-permute-start.28
  82.5 1.3 collective-permute-start.33
  83.8 0.7 collective-permute-start.30
  84.5 1.3 collective-permute-start.32
  85.8 0.3 shard_map.53
  86.1 1.8 %collective-permute-start.26 = (f32[2,384,512]{2,1,0:T(8,128)S(1)}, f32[2,384,512]{2,1,0:T(8,128)S(1)}, u32[]{:S(2)}, u32[]{:S(2)}) collective-permute-start(f32[2,384,512]{2,1,0:T(8,128)S(1)} %get-tuple-element.60), channel_id=1, source_target_pairs={{0,24},{1,29},{2,30},{3,27},{4,28},{5,25},{6,26},{7,31},{8,51},{9,... | collective-permute-start | bytes 4718600 | tf_op jit(solution)/shard_map/ppermute | solution.py:62
  88.0 38.2 %collective-permute-done.33.back_im = f32[384,512]{1,0:T(8,128)S(1)} collective-permute-done((f32[384,512]{1,0:T(8,128)S(1)}, f32[384,512]{1,0:T(8,128)S(1)}, u32[]{:S(2)}, u32[]{:S(2)}) %collective-permute-start.33) | collective-permute-done | bytes 786464 | tf_op jit(solution)/shard_map/ppermute | solution.py:58
  126.2 1.4 collective-permute-start.27
  127.6 1.3 collective-permute-start.24
  128.9 1.3 collective-permute-start.29
  130.2 1.3 collective-permute-start.31
  131.5 11.6 %collective-permute-done.29.hop_re = f32[384,512]{1,0:T(8,128)S(1)} collective-permute-done((f32[384,512]{1,0:T(8,128)S(1)}, f32[384,512]{1,0:T(8,128)S(1)}, u32[]{:S(2)}, u32[]{:S(2)}) %collective-permute-start.29) | collective-permute-done | bytes 786464 | tf_op jit(solution)/shard_map/ppermute | solution.py:58
  143.1 8.4 %collective-permute-done.31.hop_im = f32[384,512]{1,0:T(8,128)S(1)} collective-permute-done((f32[384,512]{1,0:T(8,128)S(1)}, f32[384,512]{1,0:T(8,128)S(1)}, u32[]{:S(2)}, u32[]{:S(2)}) %collective-permute-start.31) | collective-permute-done | bytes 786464 | tf_op jit(solution)/shard_map/ppermute | solution.py:58
  151.6 1.8 %shard_map.54 = f32[2,384,1024]{2,1,0:T(8,128)} custom-call(f32[2,384,512]{2,1,0:T(8,128)S(1)} %collective-permute-done.23.early, f32[2,384,512]{2,1,0:T(8,128)S(1)} %collective-permute-done.24.lowered, f32[2,384,512]{2,1,0:T(8,128)S(1)} %collective-permute-done.26.back_a, f32[2,384,512]{2,1,0:T(8,128)S(1)} %collective-permute-done.27.back_b, ...), custom_call_target="tpu_custom_call" | custom-call | tf_op jit(solution)/shard_map/pallas_call | solution.py:275
  (15 shorter events, 0.0 us)
Async XLA Ops:
  0.0 42.1 %collective-permute-start.18 = (f32[2,384,1024]{2,1,0:T(8,128)}, f32[2,384,1024]{2,1,0:T(8,128)S(1)}, u32[]{:S(2)}, u32[]{:S(2)}) collective-permute-start(f32[2,384,1024]{2,1,0:T(8,128)} %bitcast.5), channel_id=1, source_target_pairs={{0,25},{1,26},{2,95},{3,24},{4,29},{5,30},{6,91},{7,28},{8,48},{9,... | collective-permute-start | bytes 9437192 | tf_op jit(solution)/shard_map/ppermute | solution.py:58
  5.1 43.4 %collective-permute-start.20 = (f32[2,384,1024]{2,1,0:T(8,128)}, f32[2,384,1024]{2,1,0:T(8,128)}, u32[]{:S(2)}, u32[]{:S(2)}) collective-permute-start(f32[2,384,1024]{2,1,0:T(8,128)} %bitcast.6), channel_id=1, source_target_pairs={{0,3},{1,4},{2,1},{3,2},{4,7},{5,0},{6,5},{7,6},{16,19},{17,84},{1... | collective-permute-start | bytes 9437192 | tf_op jit(solution)/shard_map/ppermute | solution.py:58
  9.7 32.4 %collective-permute-start.7 = (f32[1,128]{1,0:T(1,128)}, f32[1,128]{1,0:T(1,128)}, u32[]{:S(2)}, u32[]{:S(2)}) collective-permute-start(f32[1,128]{1,0:T(1,128)} %param.3), channel_id=1, source_target_pairs={{0,118},{1,115},{2,52},{3,113},{4,114},{5,119},{6,48},{7,117},{8,1... | collective-permute-start | bytes 1544 | tf_op jit(solution)/shard_map/cond/branch_3_fun/ppermute | solution.py:58
  12.0 30.0 %collective-permute-start.6 = (f32[1,128]{1,0:T(1,128)}, f32[1,128]{1,0:T(1,128)}, u32[]{:S(2)}, u32[]{:S(2)}) collective-permute-start(f32[1,128]{1,0:T(1,128)} %param.3), channel_id=1, source_target_pairs={{0,76},{1,73},{2,74},{3,79},{4,72},{5,77},{6,78},{7,75},{8,103},{9... | collective-permute-start | bytes 1544 | tf_op jit(solution)/shard_map/cond/branch_3_fun/ppermute | solution.py:58
  42.1 12.5 %collective-permute-start.19 = (f32[2,384,1024]{2,1,0:T(8,128)S(1)}, f32[2,384,1024]{2,1,0:T(8,128)S(1)}, u32[]{:S(2)}, u32[]{:S(2)}) collective-permute-start(f32[2,384,1024]{2,1,0:T(8,128)S(1)} %collective-permute-done.18.if_lower.if_upper), channel_id=1, source_target_pairs={{0,8},{1,9},{2,10},{3,11},{4,12},{5,13},{6,14},{7,15},{16,24},{17,... | collective-permute-start | bytes 9437192 | tf_op jit(solution)/shard_map/ppermute | solution.py:58
  43.5 6.9 %collective-permute-start.22 = (f32[1,8]{1,0:T(1,128)}, f32[1,8]{1,0:T(1,128)S(1)}, u32[]{:S(2)}, u32[]{:S(2)}) collective-permute-start(f32[1,8]{1,0:T(1,128)} %bitcast.16), channel_id=1, source_target_pairs={{0,3},{1,4},{2,1},{3,2},{4,7},{5,0},{6,5},{7,6},{8,56},{9,125},{10... | collective-permute-start | bytes 104 | tf_op jit(solution)/shard_map/ppermute | solution.py:58
  48.5 5.2 %collective-permute-start.21 = (f32[1,8]{1,0:T(1,128)}, f32[1,8]{1,0:T(1,128)S(1)}, u32[]{:S(2)}, u32[]{:S(2)}) collective-permute-start(f32[1,8]{1,0:T(1,128)} %bitcast.17), channel_id=1, source_target_pairs={{0,25},{1,26},{2,95},{3,24},{4,29},{5,30},{6,91},{7,28},{8,48},{9,... | collective-permute-start | bytes 104 | tf_op jit(solution)/shard_map/ppermute | solution.py:58
  74.9 10.9 %collective-permute-start.25 = (f32[2,384,512]{2,1,0:T(8,128)S(1)}, f32[2,384,512]{2,1,0:T(8,128)S(1)}, u32[]{:S(2)}, u32[]{:S(2)}) collective-permute-start(f32[2,384,512]{2,1,0:T(8,128)S(1)} %get-tuple-element.57), channel_id=1, source_target_pairs={{0,8},{1,9},{2,10},{3,11},{4,12},{5,13},{6,14},{7,15},{8,0},{9,1},... | collective-permute-start | bytes 4718600 | tf_op jit(solution)/shard_map/ppermute | solution.py:58
  75.0 52.6 %collective-permute-start.23 = (f32[2,384,512]{2,1,0:T(8,128)S(1)}, f32[2,384,512]{2,1,0:T(8,128)S(1)}, u32[]{:S(2)}, u32[]{:S(2)}) collective-permute-start(f32[2,384,512]{2,1,0:T(8,128)S(1)} %get-tuple-element.50), channel_id=1, source_target_pairs={{0,13},{1,10},{2,11},{3,8},{4,9},{5,14},{6,15},{7,12},{8,51},{9,48... | collective-permute-start | bytes 4718600 | tf_op jit(solution)/shard_map/ppermute | solution.py:58
  81.7 2.7 %collective-permute-start.28 = (f32[384,512]{1,0:T(8,128)S(1)}, f32[384,512]{1,0:T(8,128)S(1)}, u32[]{:S(2)}, u32[]{:S(2)}) collective-permute-start(f32[384,512]{1,0:T(8,128)S(1)} %get-tuple-element.58.re), channel_id=1, source_target_pairs={{0,4},{4,0},{11,55},{15,51},{16,84},{17,88},{20,80},{21,92},{27,95... | collective-permute-start | bytes 2359304 | tf_op jit(solution)/shard_map/ppermute | solution.py:58
  82.5 43.8 %collective-permute-start.33 = (f32[384,512]{1,0:T(8,128)S(1)}, f32[384,512]{1,0:T(8,128)S(1)}, u32[]{:S(2)}, u32[]{:S(2)}) collective-permute-start(f32[384,512]{1,0:T(8,128)S(1)} %get-tuple-element.59.im), channel_id=1, source_target_pairs={{11,54},{15,50},{17,82},{21,86},{75,118},{79,114},{81,18},{85,22}} | collective-permute-start | bytes 2359304 | tf_op jit(solution)/shard_map/ppermute | solution.py:58
  83.8 45.2 %collective-permute-start.30 = (f32[384,512]{1,0:T(8,128)S(1)}, f32[384,512]{1,0:T(8,128)S(1)}, u32[]{:S(2)}, u32[]{:S(2)}) collective-permute-start(f32[384,512]{1,0:T(8,128)S(1)} %get-tuple-element.59.im), channel_id=1, source_target_pairs={{0,4},{4,0},{16,84},{20,80},{27,95},{31,91},{32,100},{36,96},{43,1... | collective-permute-start | bytes 2359304 | tf_op jit(solution)/shard_map/ppermute | solution.py:58
  84.5 45.7 %collective-permute-start.32 = (f32[384,512]{1,0:T(8,128)S(1)}, f32[384,512]{1,0:T(8,128)S(1)}, u32[]{:S(2)}, u32[]{:S(2)}) collective-permute-start(f32[384,512]{1,0:T(8,128)S(1)} %collective-permute-done.28), channel_id=1, source_target_pairs={{24,18},{28,22},{51,50},{55,54},{88,82},{92,86},{115,114},{119,118}} | collective-permute-start | bytes 2359304 | tf_op jit(solution)/shard_map/ppermute | solution.py:58
  86.1 65.4 %collective-permute-start.26 = (f32[2,384,512]{2,1,0:T(8,128)S(1)}, f32[2,384,512]{2,1,0:T(8,128)S(1)}, u32[]{:S(2)}, u32[]{:S(2)}) collective-permute-start(f32[2,384,512]{2,1,0:T(8,128)S(1)} %get-tuple-element.60), channel_id=1, source_target_pairs={{0,24},{1,29},{2,30},{3,27},{4,28},{5,25},{6,26},{7,31},{8,51},{9,... | collective-permute-start | bytes 4718600 | tf_op jit(solution)/shard_map/ppermute | solution.py:62
  126.2 25.3 %collective-permute-start.27 = (f32[2,384,512]{2,1,0:T(8,128)S(1)}, f32[2,384,512]{2,1,0:T(8,128)S(1)}, u32[]{:S(2)}, u32[]{:S(2)}) collective-permute-start(f32[2,384,512]{2,1,0:T(8,128)S(1)} %get-tuple-element.61), channel_id=1, source_target_pairs={{1,2},{2,3},{3,0},{5,6},{6,7},{7,4},{8,24},{9,29},{10,30},{11,27},... | collective-permute-start | bytes 4718600 | tf_op jit(solution)/shard_map/ppermute | solution.py:62
  127.6 24.0 %collective-permute-start.24 = (f32[2,384,512]{2,1,0:T(8,128)S(1)}, f32[2,384,512]{2,1,0:T(8,128)S(1)}, u32[]{:S(2)}, u32[]{:S(2)}) collective-permute-start(f32[2,384,512]{2,1,0:T(8,128)S(1)} %collective-permute-done.23.early), channel_id=1, source_target_pairs={{8,0},{9,1},{10,2},{11,3},{12,4},{13,5},{14,6},{15,7},{24,16},{25,... | collective-permute-start | bytes 4718600 | tf_op jit(solution)/shard_map/ppermute | solution.py:58
  128.9 14.2 %collective-permute-start.29 = (f32[384,512]{1,0:T(8,128)S(1)}, f32[384,512]{1,0:T(8,128)S(1)}, u32[]{:S(2)}, u32[]{:S(2)}) collective-permute-start(f32[384,512]{1,0:T(8,128)S(1)} %collective-permute-done.28), channel_id=1, source_target_pairs={{0,1},{4,5},{16,17},{20,21},{27,2},{31,6},{32,33},{36,37},{43,18},... | collective-permute-start | bytes 2359304 | tf_op jit(solution)/shard_map/ppermute | solution.py:58
  130.2 21.3 %collective-permute-start.31 = (f32[384,512]{1,0:T(8,128)S(1)}, f32[384,512]{1,0:T(8,128)S(1)}, u32[]{:S(2)}, u32[]{:S(2)}) collective-permute-start(f32[384,512]{1,0:T(8,128)S(1)} %collective-permute-done.30), channel_id=1, source_target_pairs={{0,1},{4,5},{16,17},{20,21},{27,2},{31,6},{32,33},{36,37},{43,18},... | collective-permute-start | bytes 2359304 | tf_op jit(solution)/shard_map/ppermute | solution.py:58
